TPU v7x, 256 devices: a whole 4x4x8 slice. The times are simulated.
256 devices in a mesh: grp: 4 (over y), seq: 32 (over z, x), tp: 2 (over core).
Axes of the slice: x: 4, y: 4, z: 8, core: 2. Of those that a mesh axis runs over, the one named last changes fastest.
Arguments:
- hidden_in: bfloat16 [4, 16384, 1792], P('grp', 'seq'), may hold values from -8 to 8
- norm_gain: float32 [1792], replicated, may hold values from 0.5 to 1.5
- w_feature: bfloat16 [1792, 256], P(None, 'tp'), may hold values from -0.125 to 0.125
- w_value: bfloat16 [1792, 1792], P(None, 'tp'), may hold values from -0.125 to 0.125
- w_window: bfloat16 [1792, 1792], P(None, 'tp'), may hold values from -0.125 to 0.125
- w_out: bfloat16 [1792, 1792], P('tp'), may hold values from -0.125 to 0.125
- prefix_state: float32 [4, 32, 8, 153, 112], P('grp', 'seq', 'tp'), may hold values from -36864 to 36864
- prefix_norm: float32 [4, 32, 8, 153], P('grp', 'seq', 'tp'), may hold values from -409.6 to 8192, as said below
- prefix_kv: bfloat16 [4, 32, 64, 1792], P('grp', 'seq', None, 'tp'), may hold values from -6 to 6
- lengths: int32 [4, 8], P('grp'), may hold values from 1 to 8192, 16384 in all within a row
- prefix_owner: int32 [4], replicated, may hold values from 0 to 31
- row_group: int32 [4], replicated, may hold values from 0 to 3, each once
Outputs:
- hidden_out: float32 [4, 16384, 1792], P('grp', 'seq', 'tp')
Inputs may be any that keep to these rules, and one draw needn't show every extreme that they name: `lengths`: each row sums to 16384 and its largest length is exactly 8192. `prefix_owner`: a slot index along seq. `row_group`: a permutation of the groups. `prefix_norm`: the first entry of each row is 8192, the count of prefix tokens; phi(q) . prefix_norm is positive for every query q.
All inputs are finite; a program needn't handle non-finite values.
Results may differ from a plain program's by a relative error of at most 0.0017.
Values may be sent and summed in bfloat16 or wider, within the bound.
A program may use at most 256 MiB of HBM per device.

v0:
```python
import math

import jax
import jax.numpy as jnp
import numpy as np
from jax import lax
from jax.sharding import PartitionSpec as P

epsilon = 1e-05
highest = lax.Precision.HIGHEST


def spread(value, axis, source):
    kept = jnp.where(lax.axis_index(axis) == source, value, 0).astype(value.dtype)
    return lax.psum(kept, axis)


def carried_in(shard, axis, combine, identity):
    devices, mine = (lax.axis_size(axis), lax.axis_index(axis))
    everything = jax.tree.map(lambda part: lax.all_gather(part, axis), shard)
    start = jax.tree.map(
        lambda part, zero: jnp.broadcast_to(jnp.asarray(zero, part.dtype), part.shape),
        shard,
        identity,
    )

    def step(k, before):
        reached = k < mine
        new = combine(before, jax.tree.map(lambda part: part[k], everything))
        return jax.tree.map(lambda a, b: jnp.where(reached, a, b), new, before)

    return lax.fori_loop(0, devices, step, start)


def passed_along(value, axis, steps):
    count = lax.axis_size(axis)
    leading, last = (max(0, -steps), min(count, count - steps))
    return lax.ppermute(value, axis, [(source, source + steps) for source in range(leading, last)])


def taylor(x):
    width = x.shape[-1]
    first_idx, second_idx = np.triu_indices(width)
    pair_weight = np.where(
        first_idx == second_idx, 1.0 / math.sqrt(2.0 * width), 1.0 / math.sqrt(width)
    ).astype(np.float32)
    unit_col = jnp.ones(x.shape[:-1] + (1,), jnp.float32)
    return jnp.concatenate(
        [unit_col, x * (1.0 / width**0.25), x[..., first_idx] * x[..., second_idx] * pair_weight],
        axis=-1,
    )


def request_start(places, starts):
    return jnp.max(jnp.where(starts[None, :] <= places[:, None], starts[None, :], 0), axis=1)


def linear_block(
    query_feat,
    key_feat,
    lin_vals,
    starts_tok,
    places,
    base_state,
    base_norm,
    carried_state,
    carried_norm,
    use_carry,
):
    phi_query = taylor(query_feat)
    value_full = lin_vals.astype(jnp.float32)
    numerator = jnp.einsum("thf,hfd->thd", phi_query, base_state, precision=highest) + use_carry[
        :, None, None
    ] * jnp.einsum("thf,hfd->thd", phi_query, carried_state, precision=highest)
    denominator = jnp.einsum("thf,hf->th", phi_query, base_norm, precision=highest) + use_carry[
        :, None
    ] * jnp.einsum("thf,hf->th", phi_query, carried_norm, precision=highest)
    similar = jnp.einsum("thf,shf->hts", query_feat, key_feat, precision=highest) * (
        1.0 / math.sqrt(query_feat.shape[-1])
    )
    allowed = (starts_tok[:, None] == starts_tok[None, :]) & (places[None, :] <= places[:, None])
    kernel = jnp.where(allowed[None], 1.0 + similar + 0.5 * similar * similar, 0.0)
    numerator = numerator + jnp.einsum("hts,shd->thd", kernel, value_full, precision=highest)
    denominator = denominator + jnp.transpose(jnp.sum(kernel, axis=2))
    return (numerator / denominator[:, :, None]).astype(jnp.bfloat16)


def block_state(key_feat, lin_vals, in_range):
    phi_key = taylor(key_feat) * in_range[:, None, None]
    state_sum = jnp.einsum("thf,thd->hfd", phi_key, lin_vals.astype(jnp.float32), precision=highest)
    return (state_sum, jnp.sum(phi_key, axis=0))


def window_block(
    win_query,
    win_keys,
    win_vals,
    rim_keys,
    rim_vals,
    prefix_keys,
    prefix_vals,
    starts_tok,
    places,
    anchor,
):
    span = prefix_keys.shape[0]
    key_rows = jnp.concatenate([prefix_keys, rim_keys, win_keys], axis=0)
    value_rows = jnp.concatenate([prefix_vals, rim_vals, win_vals], axis=0)
    later = jnp.arange(span + places.shape[0], dtype=jnp.int32) + (anchor - span)
    band = (
        (later[None, :] <= places[:, None])
        & (later[None, :] > places[:, None] - span)
        & (later[None, :] >= starts_tok[:, None])
    )
    early = jnp.arange(span, dtype=jnp.int32)[None, :] >= (places - starts_tok)[:, None] + 1
    allowed = jnp.concatenate([early, band], axis=1)
    scores = jnp.einsum("thd,khd->htk", win_query, key_rows, preferred_element_type=jnp.float32) * (
        1.0 / math.sqrt(win_query.shape[-1])
    )
    scores = jnp.where(allowed[None], scores, -1e30)
    top_score = jnp.max(scores, axis=2, keepdims=True)
    weights = jnp.exp(scores - top_score)
    weights = (weights / jnp.sum(weights, axis=2, keepdims=True)).astype(jnp.bfloat16)
    return jnp.einsum(
        "htk,khd->thd", weights, value_rows, preferred_element_type=jnp.float32
    ).astype(jnp.bfloat16)


def select_row(array, chosen):
    return lax.dynamic_index_in_dim(array, chosen, 0, keepdims=False)


def local(
    hidden_in,
    norm_gain,
    w_feature,
    w_value,
    w_window,
    w_out,
    prefix_state,
    prefix_norm,
    prefix_kv,
    lengths,
    prefix_owner,
    row_group,
):
    local_heads = prefix_state.shape[2]
    head_size = w_out.shape[0] // (2 * local_heads)
    local_rows = hidden_in.shape[1]
    span = prefix_kv.shape[2]
    grp_index = lax.axis_index("grp")
    seq_index = lax.axis_index("seq")
    anchor = seq_index * local_rows
    cache_wide = prefix_kv.astype(jnp.float32)
    chosen = row_group[grp_index]
    state_sum, norm_sum, cache_rows = (
        spread(prefix_state, "seq", prefix_owner[grp_index]),
        spread(prefix_norm, "seq", prefix_owner[grp_index]),
        spread(cache_wide, "seq", prefix_owner[grp_index]),
    )
    state_sum, norm_sum, cache_rows = (
        lax.all_gather(state_sum, "grp", axis=0, tiled=True),
        lax.all_gather(norm_sum, "grp", axis=0, tiled=True),
        lax.all_gather(cache_rows, "grp", axis=0, tiled=True),
    )
    state_sum = select_row(state_sum, chosen)
    norm_sum = select_row(norm_sum, chosen)
    cache_rows = select_row(cache_rows, chosen)
    base_state = state_sum[0]
    base_norm = norm_sum[0]
    cache_rows = cache_rows[0].astype(jnp.bfloat16).reshape(span, local_heads, 2, head_size)
    x = hidden_in[0].astype(jnp.float32)
    inv_rms = lax.rsqrt(jnp.mean(x * x, axis=1, keepdims=True) + epsilon)
    normed = (x * inv_rms * norm_gain).astype(jnp.bfloat16)
    features = jnp.dot(normed, w_feature, preferred_element_type=jnp.float32).reshape(
        local_rows, local_heads, 2, -1
    )
    values = (
        jnp.dot(normed, w_value, preferred_element_type=jnp.float32)
        .astype(jnp.bfloat16)
        .reshape(local_rows, local_heads, 2, head_size)
    )
    window = (
        jnp.dot(normed, w_window, preferred_element_type=jnp.float32)
        .astype(jnp.bfloat16)
        .reshape(local_rows, local_heads, 2, head_size)
    )
    query_feat = features[:, :, 0]
    key_feat = features[:, :, 1]
    lin_vals = values[:, :, 0]
    win_vals = values[:, :, 1]
    win_query = window[:, :, 0]
    win_keys = window[:, :, 1]
    lengths_row = lengths[0]
    starts = jnp.cumsum(lengths_row) - lengths_row
    places = anchor + jnp.arange(local_rows, dtype=jnp.int32)
    starts_tok = request_start(places, starts)
    zero_state = jnp.zeros(base_state.shape, jnp.float32)
    zero_norm = jnp.zeros(base_norm.shape, jnp.float32)
    in_last = (starts_tok == starts_tok[-1]).astype(jnp.float32)
    part_state, part_norm = block_state(key_feat, lin_vals, in_last)
    restart = (starts_tok[-1] >= anchor).astype(jnp.float32)

    def combine(earlier, later):
        keep_earlier = 1.0 - later[2]
        return (
            keep_earlier * earlier[0] + later[0],
            keep_earlier * earlier[1] + later[1],
            jnp.maximum(earlier[2], later[2]),
        )

    carried_state, carried_norm, _ = carried_in(
        (part_state, part_norm, restart),
        "seq",
        combine,
        (zero_state, zero_norm, jnp.zeros((), jnp.float32)),
    )
    use_carry = (starts_tok < anchor).astype(jnp.float32)
    lin_out = linear_block(
        query_feat,
        key_feat,
        lin_vals,
        starts_tok,
        places,
        base_state,
        base_norm,
        carried_state,
        carried_norm,
        use_carry,
    )
    own_pairs = jnp.stack([win_keys, win_vals], axis=2).reshape(
        local_rows, local_heads * 2 * head_size
    )
    rim_rows = passed_along(own_pairs[local_rows - span :], "seq", 1).reshape(
        span, local_heads, 2, head_size
    )
    win_out = window_block(
        win_query,
        win_keys,
        win_vals,
        rim_rows[:, :, 0],
        rim_rows[:, :, 1],
        cache_rows[:, :, 0],
        cache_rows[:, :, 1],
        starts_tok,
        places,
        anchor,
    )
    attended = jnp.stack([lin_out, win_out], axis=2).reshape(
        local_rows, local_heads * 2 * head_size
    )
    columns = hidden_in.shape[2] // lax.axis_size("tp")
    column_start = lax.axis_index("tp") * columns
    mixed_out = jnp.dot(attended, w_out, preferred_element_type=jnp.float32)
    summed = lax.psum_scatter(mixed_out, "tp", scatter_dimension=1, tiled=True)
    residual = lax.dynamic_slice_in_dim(hidden_in[0], column_start, columns, 1).astype(jnp.float32)
    return (residual + summed)[None]


def solution(mesh):
    placed = (
        P("grp", "seq", None),
        P(),
        P(None, "tp"),
        P(None, "tp"),
        P(None, "tp"),
        P("tp", None),
        P("grp", "seq", "tp", None, None),
        P("grp", "seq", "tp", None),
        P("grp", "seq", None, "tp"),
        P("grp", None),
        P(),
        P(),
    )
    return jax.shard_map(
        local, mesh=mesh, in_specs=placed, out_specs=P("grp", "seq", "tp"), check_vma=False
    )
```

profile of v0, /device:TPU:1, one launch (start us, length us, event | category | flops | bytes accessed | tf_op | source)
XLA Modules:
  0.0 605.8 jit_solution(7075174274370640115)
XLA Ops:
  6.5 1.4 dynamic_slice.45
  11.0 1.9 fusion.6
  12.9 2.0 copy.80
  15.0 2.4 fusion.24
  18.8 137.2 %all-reduce.5.cloned.1.call-done = f32[1,1,4,153,112]{4,2,3,1,0:T(4,128)} async-done(((f32[1,1,4,153,112]{4,2,3,1,0:T(4,128)}), f32[1,1,4,153,112]{4,2,3,1,0:T(4,128)}) %all-reduce.5.cloned.1.call-update) | async-done | bytes 274192 | tf_op jit(solution)/shard_map/psum | solution.py:15
  157.1 2.4 gather_fusion
  159.5 2.3 gather_fusion.1
  161.9 2.3 gather_fusion.2
  164.2 2.3 gather_fusion.3
  167.2 5.5 convolution_convert_fusion.1
  172.7 2.3 copy.90
  176.3 4.6 fusion.36
  182.0 1.7 fusion.38
  183.7 5.5 convolution_convert_fusion
  189.2 2.2 copy.94
  191.5 1.9 slice_bitcast_fusion.5
  193.3 1.9 slice_bitcast_fusion.8
  196.2 1.7 slice.48
  197.9 3.4 collective-permute-start
  204.5 1.6 convert_select_fusion
  208.6 2.0 dynamic-update-slice
  211.1 117.2 %all-reduce.6 = (bf16[1,1,64,896]{3,2,1,0:T(8,128)(2,1)}, f32[32]{0:T(128)}, f32[1,1,4,153]{3,2,1,0:T(4,128)}) all-reduce(f32[1,1,64,896]{3,2,1,0:T(8,128)} %convert_select_fusion, f32[32]{0:T(128)} %dynamic-update-slice, f32[1,1,4,153]{3,2,1,0:T(4,128)} %broadcast_select_fusion.1), channel_id=1, replica_groups=mesh['grp'=4,'seq'=32,'tp'=2] {'seq'}, use_global_device_ids=true, to_apply=%region_9.10 | all-reduce | flops 57988 | bytes 349216 | tf_op jit(solution)/shard_map/psum | solution.py:15
  328.3 11.1 %all_gather.39 = bf16[4,1,64,896]{3,2,1,0:T(8,128)(2,1)S(1)} all-gather(bf16[1,1,64,896]{3,2,1,0:T(8,128)(2,1)} %get-tuple-element.170), channel_id=1, replica_groups=mesh['grp'=4,'seq'=32,'tp'=2] {'grp'}, dimensions={0}, use_global_device_ids=true | all-gather | bytes 573440 | tf_op jit(solution)/shard_map/all_gather | solution.py:164
  340.0 1.7 convert_element_type.92
  341.8 1.9 fusion.74
  343.7 1.7 copy.116
  345.4 1.7 copy.111
  347.0 9.7 %all_gather.38 = f32[4,1,4,153]{3,2,1,0:T(4,128)S(1)} all-gather(f32[1,1,4,153]{3,2,1,0:T(4,128)} %get-tuple-element.172), channel_id=1, replica_groups=mesh['grp'=4,'seq'=32,'tp'=2] {'grp'}, dimensions={0}, use_global_device_ids=true | all-gather | bytes 12240 | tf_op jit(solution)/shard_map/all_gather | solution.py:163
  356.7 1.6 fusion.37
  358.3 35.5 %all-gather.2 = f32[32,4,153]{2,1,0:T(4,128)} all-gather(f32[1,4,153]{2,1,0:T(4,128)S(1)} %bitcast.157), channel_id=3, replica_groups=mesh['grp'=4,'seq'=32,'tp'=2] {'seq'}, dimensions={0}, use_global_device_ids=true | all-gather | bytes 80784 | tf_op jit(solution)/shard_map/all_gather | solution.py:20
  393.8 2.8 fusion.61
  397.4 5.1 fusion.11
  402.5 3.5 fusion.12
  407.2 1.7 reshape.156
  408.9 1.9 fusion.75
  410.8 1.7 copy.117
  412.5 1.7 copy.114
  414.1 2.2 fusion.46
  416.4 2.9 fusion.76
  419.3 1.9 fusion.31
  421.2 1.7 constant_dynamic-slice_fusion
  422.9 101.0 %while.16 = (s32[]{:T(128)}, f32[4,153,112]{2,1,0:T(8,128)S(1)}, f32[4,153]{1,0:T(4,128)S(1)}, s32[]{:T(128)}, f32[32]{0:T(128)S(1)}, /*index=5*/f32[32,4,153,11...) while((s32[]{:T(128)}, f32[4,153,112]{2,1,0:T(8,128)S(1)}, ...), condition=%wide.region_6.7_spmd.clone, body=%wide.region_5.6_spmd.clone.sunk | while | flops 276629 | bytes 830035 | solution.py:32
  524.0 2.3 fusion.59
  526.3 2.1 convolution_multiply_fusion
  528.5 1.3 fusion.32
  530.0 3.9 fusion.77
  534.0 62.1 %reduce-scatter.2.cloned.1.call-done = f32[512,896]{1,0:T(8,128)} async-done(((f32[512,1792]{1,0:T(8,128)}), f32[512,896]{1,0:T(8,128)}) %reduce-scatter.2.cloned.1.call-update) | async-done | bytes 1835024 | tf_op jit(solution)/shard_map/reduce_scatter | solution.py:255
  596.1 3.1 fusion.23
  (195 shorter events, 94.4 us)
Async XLA Ops:
  6.5 523.5 %copy-start = (bf16[896,1792]{1,0:T(8,128)(2,1)S(1)}, bf16[896,1792]{1,0:T(8,128)(2,1)}, u32[]{:S(2)}) copy-start(bf16[896,1792]{1,0:T(8,128)(2,1)} %param.29) | copy-start | bytes 9633796
  6.5 149.5 %all-reduce.5.cloned.1.call-start = ((), (), s32[]{:S(2)}) async-start(), calls=%async_computation.1 | async-start | bytes 626688 | tf_op jit(solution)/shard_map/psum | solution.py:15
  8.6 6.4 %copy-start.24 = (f32[1792]{0:T(1024)S(1)}, f32[1792]{0:T(1024)}, u32[]{:S(2)}) copy-start(f32[1792]{0:T(1024)} %param.25) | copy-start | bytes 21508
  9.4 411.8 %all-gather.6.cloned.1.call-start = ((), (), s32[]{:S(2)}) async-start(), calls=%async_computation.2 | async-start | bytes 1566720 | tf_op jit(solution)/shard_map/all_gather | solution.py:162
  15.0 2.4 copy-start.22
  15.0 141.1 %copy-start.21 = (s32[136]{0:T(256)S(1)}, s32[136]{0:T(256)}, u32[]{:S(2)}) copy-start(s32[136]{0:T(256)} %constant.126) | copy-start | bytes 1636
  17.4 0.7 copy-start.5
  156.1 266.8 %all-gather.8.cloned.1.call-start = ((), (), s32[]{:S(2)}) async-start(), calls=%async_computation.4 | async-start | bytes 10813440 | tf_op jit(solution)/shard_map/all_gather | solution.py:20
  172.7 2.9 copy-start.6
  172.7 3.6 copy-start.23
  175.0 6.0 copy-start.16
  175.7 5.3 copy-start.18
  176.3 4.7 copy-start.8
  176.3 5.6 copy-start.3
  181.0 1.0 copy-start.1
  183.7 412.4 %reduce-scatter.2.cloned.1.call-start = ((), (), s32[]{:S(2)}) async-start(), calls=%async_computation.3 | async-start | bytes 5505024 | tf_op jit(solution)/shard_map/reduce_scatter | solution.py:255
  197.9 209.3 %collective-permute-start = (bf16[64,896]{1,0:T(8,128)(2,1)}, bf16[64,896]{1,0:T(8,128)(2,1)}, u32[]{:S(2)}, u32[]{:S(2)}) collective-permute-start(bf16[64,896]{1,0:T(8,128)(2,1)} %slice.48), channel_id=1, source_target_pairs={{0,2},{2,4},{4,6},{6,8},{8,10},{10,12},{12,14},{14,16},{16,18},{18... | collective-permute-start | bytes 344072 | tf_op jit(solution)/shard_map/ppermute | solution.py:38
  347.0 50.4 %copy-start.7 = (f32[512,4,2,16]{0,3,2,1:T(8,128)S(1)}, f32[512,4,2,16]{0,3,2,1:T(8,128)}, u32[]{:S(2)}) copy-start(f32[512,4,2,16]{0,3,2,1:T(8,128)} %copy-done.5) | copy-start | bytes 786436
  397.4 5.1 copy-start.4
  414.1 2.2 copy-start.12
  416.3 2.9 copy-start.11
  416.3 2.9 copy-start.14
  416.3 2.9 copy-start.15
  419.3 3.6 copy-start.25
  422.9 101.0 %copy-start.17 = (f32[153]{0:T(256)S(1)}, f32[153]{0:T(256)}, u32[]{:S(2)}) copy-start(f32[153]{0:T(256)} %copy-done.16) | copy-start | bytes 1840
  523.9 2.4 copy-start.2
  523.9 4.5 copy-start.19
  523.9 4.5 copy-start.20
  523.9 4.5 copy-start.9
  524.0 4.5 copy-start.13
  524.0 4.5 copy-start.26
  528.5 1.4 copy-start.10
Sparse Core Ops, SparseCore 0:
  10.8 145.1 all-reduce.4
  157.8 27.7 all-gather.5
  188.2 111.4 all-gather.7
  534.1 61.9 reduce-scatter.1
where the time goes:
time: 609 us; the launch traced here: 606 us
  waiting for transfers between devices  199 us (33%)
  blocking collectives  173 us (28%)
  other arithmetic  80.5 us (13%)
  local copies, waits for them, and re-layouts  69.9 us (11%)
  matrix products  40.2 us (7%)
  loops' own time  22.1 us (4%)
  between operations  16.7 us (3%)
    psum x1, waiting for transfers between devices, spread(): return lax.psum(kept, axis)  137 us
    psum x1, blocking collectives, spread(): return lax.psum(kept, axis)  117 us
    reduce_scatter x1, waiting for transfers between devices, local(): summed = lax.psum_scatter(mixed_out, 'tp', scatter_dimension=1, tiled=True)  62.1 us
    select_n x64, other arithmetic, step(): return jax.tree.map(lambda a, b: jnp.where(reached, a, b), new, before)  58.2 us
    all_gather x1, blocking collectives, carried_in(): everything = jax.tree.map(lambda part: lax.all_gather(part, axis), shard)  35.5 us
    another operation x1, loops' own time, carried_in(): return lax.fori_loop(0, devices, step, start)  22.1 us
    dynamic_slice x32, local copies, waits for them, and re-layouts, step(): new = combine(before, jax.tree.map(lambda part: part[k], everything))  20.7 us
    unnamed x63, local copies, waits for them, and re-layouts  16.1 us
  transfers between devices with their start and end apart: 5, of which 2 were waited for; matrix products, arithmetic and copies ran while one was open for 16% of the time, Pallas kernels for 0%

commit v1 on v0

v1 whole, which is shorter than its diff:
```python
import functools
import math

import jax
import jax.numpy as jnp
import numpy as np
from jax import lax
from jax.experimental import pallas as pl
from jax.experimental.pallas import tpu as pltpu
from jax.sharding import PartitionSpec as P

MESH = pl.DeviceIdType.MESH
LANES = 128
CHUNK = 32
KV_CHUNK = 16
f32, bf16 = jnp.float32, jnp.bfloat16


def feature_tables(heads, fd, padded):
    first, second = np.triu_indices(fd)
    count = 1 + fd + len(first)
    rows = np.zeros((8, heads * padded), np.float32)
    rows[0:4] = -1.0
    for h in range(heads):
        at = h * padded
        rows[4, at] = rows[5, at] = rows[6, at] = 1.0
        for kind in range(2):
            base = h * 2 * fd + kind * fd
            rows[2 * kind, at + 1 : at + 1 + fd] = base + np.arange(fd)
            rows[2 * kind, at + 1 + fd : at + count] = base + first
            rows[2 * kind + 1, at + 1 + fd : at + count] = base + second
        rows[5, at + 1 : at + 1 + fd] = 1.0
        rows[6, at + 1 : at + 1 + fd] = 1.0 / fd**0.25
        rows[6, at + 1 + fd : at + count] = np.where(
            first == second, 1.0 / math.sqrt(2.0 * fd), 1.0 / math.sqrt(fd)
        )
    return rows


def split_norm(x, ones_lane):
    lane = lax.broadcasted_iota(jnp.int32, x.shape, x.ndim - 1)
    lost = x - x.astype(bf16).astype(f32)
    moved = pltpu.roll(lost, 1, x.ndim - 1)
    return jnp.where(lane == ones_lane + 1, x + moved, x).astype(bf16)


def start_offsets(starts_ref, anchor, rows, first):
    place = lax.broadcasted_iota(jnp.int32, (rows, 1), 0) + (first + anchor)
    best = jnp.zeros((rows, 1), jnp.int32)
    for r in range(starts_ref.shape[0]):
        best = jnp.maximum(best, jnp.where(starts_ref[r] <= place, starts_ref[r], 0))
    return best - anchor


def project_body(
    starts_ref, hidden, gain, w_feature, w_value, w_window, state, norm, kv, tab_row, tab_col,
    phi_q, feat, feat_t, lin_vals, win_q, win_kv, cache, parts,
    normed, wide,
):
    rows, width = hidden.shape
    heads, nf, hd = state.shape
    padded = parts.shape[0] * CHUNK // heads
    anchor = lax.axis_index("seq") * rows
    per_head = padded // CHUNK
    for h in range(heads):
        body = jnp.concatenate(
            [state[h], norm[h], jnp.zeros((nf, LANES - hd - 1), f32)], axis=1
        )
        body = jnp.concatenate([body, jnp.zeros((padded - nf, LANES), f32)], axis=0)
        cache[h * per_head : (h + 1) * per_head, 0:CHUNK, :] = split_norm(body, hd).reshape(
            per_head, CHUNK, LANES
        )
    span = kv.shape[0]
    blocks = span // KV_CHUNK
    for i in range(2 * heads):
        piece = jnp.concatenate(
            [kv[:, i * hd : (i + 1) * hd], jnp.zeros((span, LANES - hd), bf16)], axis=1
        )
        cache[i * blocks : (i + 1) * blocks, CHUNK:, :] = piece.reshape(blocks, KV_CHUNK, LANES)
    step = 64

    def norm_rows(i, carry):
        at = pl.ds(pl.multiple_of(i * step, step), step)
        x = hidden[at, :].astype(f32)
        inv = lax.rsqrt(jnp.mean(x * x, axis=1, keepdims=True) + 1e-5)
        normed[at, :] = (x * inv * gain[...]).astype(bf16)
        return carry

    lax.fori_loop(0, rows // step, norm_rows, 0)
    feats = jnp.dot(normed[...], w_feature[...], preferred_element_type=f32)
    feats_t = jnp.transpose(feats)
    hi = feats.astype(bf16)
    both = jnp.concatenate([hi, (feats - hi.astype(f32)).astype(bf16)], axis=1)
    hi_t = feats_t.astype(bf16)
    both_t = jnp.concatenate([hi_t, (feats_t - hi_t.astype(f32)).astype(bf16)], axis=0)
    feat[...] = hi
    feat_t[...] = hi_t
    channels = hi.shape[1]
    total = heads * padded
    for n in range(heads):
        at = slice(n * padded, (n + 1) * padded)
        channel = (
            lax.broadcasted_iota(jnp.int32, (2 * channels, padded), 0) % channels
        ).astype(f32)
        one = jnp.where(channel == tab_row[0:1, at], 1.0, 0.0).astype(bf16)
        two = jnp.where(channel == tab_row[1:2, at], 1.0, 0.0).astype(bf16)
        left = jnp.dot(both, one, preferred_element_type=f32) + tab_row[4:5, at]
        right = jnp.dot(both, two, preferred_element_type=f32) + tab_row[5:6, at]
        phi_q[:, at] = (left * right * tab_row[6:7, at]).astype(bf16)
    for lo in range(0, w_value.shape[1], 256):
        up = min(lo + 256, w_value.shape[1])
        wide[:, lo:up] = jnp.dot(
            normed[...], w_value[:, lo:up], preferred_element_type=f32
        ).astype(bf16)
    lane = lax.broadcasted_iota(jnp.int32, (rows, LANES - hd), 1)
    ones = jnp.where(lane == 0, 1.0, 0.0).astype(bf16)
    zeros = jnp.zeros((rows, LANES - hd), bf16)
    for h in range(heads):
        at = 2 * h * hd
        lin_vals[h] = jnp.concatenate([wide[:, at : at + hd], ones], axis=1)
        win_kv[2 * h + 1] = jnp.concatenate([wide[:, at + hd : at + 2 * hd], zeros], axis=1)
    last_start = jnp.int32(0)
    for r in range(starts_ref.shape[0]):
        last_start = jnp.maximum(
            last_start, jnp.where(starts_ref[r] <= anchor + rows - 1, starts_ref[r], 0)
        )
    token = lax.broadcasted_iota(jnp.int32, (1, rows), 1)
    keep = jnp.where(token >= last_start - anchor, 1.0, 0.0)
    for h in range(heads):
        at = slice(h * padded, (h + 1) * padded)
        channel = (
            lax.broadcasted_iota(jnp.int32, (padded, 2 * channels), 1) % channels
        ).astype(f32)
        one = jnp.where(channel == tab_col[at, 2:3], 1.0, 0.0).astype(bf16)
        two = jnp.where(channel == tab_col[at, 3:4], 1.0, 0.0).astype(bf16)
        left = jnp.dot(one, both_t, preferred_element_type=f32) + tab_col[at, 4:5]
        right = jnp.dot(two, both_t, preferred_element_type=f32) + tab_col[at, 5:6]
        phi_t = (left * right * tab_col[at, 6:7] * keep).astype(bf16)
        own = jnp.dot(phi_t, lin_vals[h], preferred_element_type=f32)
        parts[h * per_head : (h + 1) * per_head] = split_norm(own, hd).reshape(
            per_head, CHUNK, LANES
        )
    for lo in range(0, w_window.shape[1], 256):
        up = min(lo + 256, w_window.shape[1])
        wide[:, lo:up] = jnp.dot(
            normed[...], w_window[:, lo:up], preferred_element_type=f32
        ).astype(bf16)
    for h in range(heads):
        at = 2 * h * hd
        win_q[h] = jnp.concatenate([wide[:, at : at + hd], zeros], axis=1)
        win_kv[2 * h] = jnp.concatenate([wide[:, at + hd : at + 2 * hd], zeros], axis=1)


def attend_body(
    starts_ref, phi_q, feat, feat_t, lin_vals, win_q, win_kv, base, carried, rim, attended,
    hd, fd,
):
    heads, rows, _ = lin_vals.shape
    span = rim.shape[1]
    per_head = base.shape[0] // heads
    padded = per_head * CHUNK
    blocks = span // KV_CHUNK
    anchor = lax.axis_index("seq") * rows
    tile = 128
    lane = lax.broadcasted_iota(jnp.int32, (tile, LANES), 1)
    for b in range(rows // tile):
        first = b * tile
        begin = start_offsets(starts_ref, anchor, tile, first)
        token = lax.broadcasted_iota(jnp.int32, (tile, 1), 0) + first
        use_carry = jnp.where(begin < 0, 1.0, 0.0)
        seen = first + tile
        key_at = lax.broadcasted_iota(jnp.int32, (tile, seen), 1)
        causal = (key_at <= token) & (key_at >= begin)
        slot = lax.broadcasted_iota(jnp.int32, (tile, 2 * span + tile), 1)
        local = slot + (first - 2 * span)
        early = (slot < span) & (slot >= token - begin + 1)
        band = (slot >= span) & (local <= token) & (local > token - span) & (local >= begin)
        visible = early | band
        at = slice(first, first + tile)
        for h in range(heads):
            q = feat[at, h * 2 * fd : h * 2 * fd + fd]
            k_t = feat_t[h * 2 * fd + fd : (h + 1) * 2 * fd, 0:seen]
            similar = jnp.dot(q, k_t, preferred_element_type=f32) * (1.0 / math.sqrt(fd))
            kernel = jnp.where(causal, 1.0 + similar + 0.5 * similar * similar, 0.0)
            mixed = jnp.dot(kernel.astype(bf16), lin_vals[h, 0:seen, :], preferred_element_type=f32)
            phi = phi_q[at, h * padded : (h + 1) * padded]
            own = slice(h * per_head, (h + 1) * per_head)
            from_base = base[own, 0:CHUNK, :].reshape(padded, LANES)
            from_carry = carried[own].reshape(padded, LANES)
            mixed = mixed + jnp.dot(phi, from_base, preferred_element_type=f32)
            mixed = mixed + use_carry * jnp.dot(phi, from_carry, preferred_element_type=f32)
            below = mixed[:, hd : hd + 1] + mixed[:, hd + 1 : hd + 2]
            lin_out = jnp.where(lane < hd, mixed / below, 0.0)
            attended[at, 2 * h * LANES : (2 * h + 1) * LANES] = lin_out.astype(bf16)
            sides = []
            for side in range(2):
                i = 2 * h + side
                cached = base[i * blocks : (i + 1) * blocks, CHUNK:, :].reshape(span, LANES)
                if b == 0:
                    sides.append(
                        jnp.concatenate([cached, rim[i], win_kv[i, 0:tile, :]], axis=0)
                    )
                else:
                    sides.append(
                        jnp.concatenate([cached, win_kv[i, first - span : first + tile, :]], axis=0)
                    )
            scores = lax.dot_general(
                win_q[h, at, :], sides[0], (((1,), (1,)), ((), ())), preferred_element_type=f32
            ) * (1.0 / math.sqrt(hd))
            scores = jnp.where(visible, scores, -1e30)
            weights = jnp.exp(scores - jnp.max(scores, axis=1, keepdims=True))
            weights = (weights / jnp.sum(weights, axis=1, keepdims=True)).astype(bf16)
            win_out = jnp.dot(weights, sides[1], preferred_element_type=f32)
            attended[at, (2 * h + 1) * LANES : (2 * h + 2) * LANES] = win_out.astype(bf16)


def exchange_body(
    hd, where_ref, keep_ref, cache, parts, win_kv, base, carried, rim,
    got_cache, got_parts, mine, got_rows, chosen, results,
    out_c, out_p, out_g, out_b, out_r, in_c, in_p, in_g, in_b, in_r, rim_sems,
):
    me, row = lax.axis_index("seq"), lax.axis_index("grp")
    count, rows = got_cache.shape[0], got_rows.shape[0]
    span, length = rim.shape[1], win_kv.shape[1]

    def seq_copy(src, dst, send, recv, peer):
        return pltpu.make_async_remote_copy(
            src_ref=src, dst_ref=dst, send_sem=send, recv_sem=recv,
            device_id={"seq": peer}, device_id_type=MESH,
        )

    def each_peer(do):
        def step(i, carry):
            do(lax.rem(me + i, count))
            return carry

        lax.fori_loop(1, count, step, 0)

    barrier = pltpu.get_barrier_semaphore()
    each_peer(
        lambda peer: pl.semaphore_signal(
            barrier, inc=1, device_id={"seq": peer}, device_id_type=MESH
        )
    )
    for i in range(1, rows):
        pl.semaphore_signal(
            barrier, inc=1, device_id={"grp": lax.rem(row + i, rows)}, device_id_type=MESH
        )
    pl.semaphore_wait(barrier, count + rows - 2)

    def part_to(peer, slot):
        return seq_copy(parts.at[peer], got_parts.at[slot], out_p.at[peer], in_p.at[slot], peer)

    def cache_to(peer, slot):
        return seq_copy(cache.at[peer], got_cache.at[slot], out_c.at[peer], in_c.at[slot], peer)

    def base_to(peer, slot):
        return seq_copy(chosen, base.at[slot], out_b.at[peer], in_b.at[slot], peer)

    def result_to(peer, slot):
        return seq_copy(results.at[peer], carried.at[slot], out_r.at[peer], in_r.at[slot], peer)

    def row_to(peer, slot):
        return pltpu.make_async_remote_copy(
            src_ref=mine, dst_ref=got_rows.at[slot], send_sem=out_g.at[peer],
            recv_sem=in_g.at[slot], device_id={"grp": peer}, device_id_type=MESH,
        )

    rim_copy = seq_copy(
        win_kv.at[:, pl.ds(length - span, span), :], rim, rim_sems.at[0], rim_sems.at[1],
        lax.rem(me + 1, count),
    )
    each_peer(lambda peer: cache_to(peer, me).start())
    each_peer(lambda peer: part_to(peer, me).start())
    rim_copy.start()
    got_cache[me] = cache[me]
    got_parts[me] = parts[me]
    each_peer(lambda peer: cache_to(peer, peer).wait_recv())
    mine[...] = got_cache[where_ref[0]]
    for i in range(1, rows):
        row_to(lax.rem(row + i, rows), row).start()
    got_rows[row] = mine[...]
    each_peer(lambda peer: part_to(peer, peer).wait_recv())

    def scan(k, total):
        results[k] = split_norm(total, hd)
        return total * keep_ref[k] + got_parts[k].astype(f32)

    lax.fori_loop(0, count, scan, jnp.zeros(parts.shape[1:], f32))
    each_peer(lambda peer: result_to(peer, me).start())
    carried[me] = results[me]
    for i in range(1, rows):
        row_to(lax.rem(row + i, rows), lax.rem(row + i, rows)).wait_recv()
    chosen[...] = got_rows[where_ref[1]]
    each_peer(lambda peer: base_to(peer, me).start())
    base[me] = chosen[...]
    each_peer(lambda peer: result_to(peer, peer).wait_recv())
    each_peer(lambda peer: base_to(peer, peer).wait_recv())
    rim_copy.wait()
    each_peer(lambda peer: cache_to(peer, me).wait_send())
    each_peer(lambda peer: part_to(peer, me).wait_send())
    each_peer(lambda peer: result_to(peer, me).wait_send())
    each_peer(lambda peer: base_to(peer, me).wait_send())
    for i in range(1, rows):
        row_to(lax.rem(row + i, rows), row).wait_send()


def output_body(attended, w_out, out, w_own, w_other, from_other, own_sem, w_send, w_recv, sems):
    me = lax.axis_index("tp")
    other = 1 - me
    half = out.shape[1]
    pieces = w_own.shape[0] // LANES
    hd = w_out.shape[0] // pieces

    def columns(which):
        return pl.ds(pl.multiple_of(which * half, LANES), half)

    barrier = pltpu.get_barrier_semaphore()
    pl.semaphore_signal(barrier, inc=1, device_id={"tp": other}, device_id_type=MESH)
    own, sent = [], []
    for i in range(pieces):
        rows, padded = slice(i * hd, (i + 1) * hd), slice(i * LANES, i * LANES + hd)
        own.append(
            pltpu.make_async_copy(
                w_out.at[rows, columns(me)], w_own.at[padded, :], own_sem.at[i]
            )
        )
        sent.append(
            pltpu.make_async_remote_copy(
                src_ref=w_out.at[rows, columns(other)], dst_ref=w_other.at[padded, :],
                send_sem=w_send.at[i], recv_sem=w_recv.at[i],
                device_id={"tp": other}, device_id_type=MESH,
            )
        )
        own[i].start()
        rest = slice(i * LANES + hd, (i + 1) * LANES)
        w_own[rest, :] = jnp.zeros((LANES - hd, half), bf16)
        w_other[rest, :] = jnp.zeros((LANES - hd, half), bf16)
    pl.semaphore_wait(barrier, 1)
    across = pltpu.make_async_remote_copy(
        src_ref=attended, dst_ref=from_other, send_sem=sems.at[0], recv_sem=sems.at[1],
        device_id={"tp": other}, device_id_type=MESH,
    )
    across.start()
    for copy in sent:
        copy.start()
    for copy in own:
        copy.wait()
    for lo in range(0, half, 256):
        up = min(lo + 256, half)
        out[:, lo:up] = jnp.dot(attended[...], w_own[:, lo:up], preferred_element_type=f32)
    for copy in sent:
        copy.wait()
    across.wait()
    for lo in range(0, half, 256):
        up = min(lo + 256, half)
        out[:, lo:up] += jnp.dot(from_other[...], w_other[:, lo:up], preferred_element_type=f32)


def local(
    hidden_in, norm_gain, w_feature, w_value, w_window, w_out,
    prefix_state, prefix_norm, prefix_kv, lengths, prefix_owner, row_group,
):
    heads, nf, hd = prefix_state.shape[2:]
    fd = w_feature.shape[1] // (2 * heads)
    rows, width = hidden_in.shape[1:]
    span = prefix_kv.shape[2]
    count, groups = lax.axis_size("seq"), lax.axis_size("grp")
    padded = count * CHUNK // heads
    grp = lax.axis_index("grp")
    row = lengths[0]
    starts = jnp.cumsum(row) - row
    first = jnp.arange(count, dtype=jnp.int32)[:, None] * rows
    fresh = jnp.any((starts[None, :] >= first) & (starts[None, :] < first + rows), axis=1)
    keep = 1.0 - fresh.astype(f32)
    where = jnp.stack([prefix_owner[grp], row_group[grp]])
    tab = feature_tables(heads, fd, padded)

    def shape(dims, dtype=bf16):
        return jax.ShapeDtypeStruct(dims, dtype)

    vmem = pl.BlockSpec(memory_space=pltpu.VMEM)
    smem = pl.BlockSpec(memory_space=pltpu.SMEM)
    dma = pltpu.SemaphoreType.DMA
    limit = 60 * 1024 * 1024
    phi_q, feat, feat_t, lin_vals, win_q, win_kv, cache, parts = pl.pallas_call(
        project_body,
        out_shape=[
            shape((rows, heads * padded)),
            shape((rows, 2 * heads * fd)),
            shape((2 * heads * fd, rows)),
            shape((heads, rows, LANES)),
            shape((heads, rows, LANES)),
            shape((2 * heads, rows, LANES)),
            shape((count, CHUNK + KV_CHUNK, LANES)),
            shape((count, CHUNK, LANES)),
        ],
        in_specs=[smem] + [vmem] * 10,
        out_specs=[vmem] * 8,
        scratch_shapes=[pltpu.VMEM((rows, width), bf16), pltpu.VMEM((rows, 2 * heads * hd), bf16)],
        compiler_params=pltpu.CompilerParams(vmem_limit_bytes=limit),
        name="project",
    )(
        starts, hidden_in[0], norm_gain[None], w_feature, w_value, w_window,
        prefix_state[0, 0], prefix_norm[0, 0][:, :, None], prefix_kv[0, 0],
        jnp.asarray(tab), jnp.asarray(np.ascontiguousarray(tab.T)),
    )
    both = CHUNK + KV_CHUNK
    base, carried, rim = pl.pallas_call(
        functools.partial(exchange_body, hd),
        out_shape=[
            shape((count, both, LANES)),
            shape((count, CHUNK, LANES)),
            shape((2 * heads, span, LANES)),
        ],
        in_specs=[smem] * 2 + [vmem] * 3,
        out_specs=[vmem] * 3,
        scratch_shapes=[
            pltpu.VMEM((count, both, LANES), bf16),
            pltpu.VMEM((count, CHUNK, LANES), bf16),
            pltpu.VMEM((both, LANES), bf16),
            pltpu.VMEM((groups, both, LANES), bf16),
            pltpu.VMEM((both, LANES), bf16),
            pltpu.VMEM((count, CHUNK, LANES), bf16),
        ]
        + [dma((count,)), dma((count,)), dma((groups,)), dma((count,)), dma((count,))] * 2
        + [dma((2,))],
        compiler_params=pltpu.CompilerParams(
            collective_id=0, has_side_effects=True, vmem_limit_bytes=limit
        ),
        name="exchange",
    )(where, keep, cache, parts, win_kv)
    attended = pl.pallas_call(
        functools.partial(attend_body, hd=hd, fd=fd),
        out_shape=shape((rows, 2 * heads * LANES)),
        in_specs=[smem] + [vmem] * 9,
        out_specs=vmem,
        compiler_params=pltpu.CompilerParams(vmem_limit_bytes=limit),
        name="attend",
    )(starts, phi_q, feat, feat_t, lin_vals, win_q, win_kv, base, carried, rim)
    columns = width // lax.axis_size("tp")
    mixed = pl.pallas_call(
        output_body,
        out_shape=shape((rows, columns), f32),
        in_specs=[vmem] * 2,
        out_specs=vmem,
        scratch_shapes=[
            pltpu.VMEM((2 * heads * LANES, columns), bf16),
            pltpu.VMEM((2 * heads * LANES, columns), bf16),
            pltpu.VMEM((rows, 2 * heads * LANES), bf16),
            dma((2 * heads,)), dma((2 * heads,)), dma((2 * heads,)), dma((2,)),
        ],
        compiler_params=pltpu.CompilerParams(
            collective_id=1, has_side_effects=True, vmem_limit_bytes=limit
        ),
        name="mix",
    )(attended, w_out)
    at = lax.axis_index("tp") * columns
    residual = lax.dynamic_slice_in_dim(hidden_in[0], at, columns, 1).astype(f32)
    return (residual + mixed)[None]


def solution(mesh):
    placed = (
        P("grp", "seq", None),
        P(),
        P(None, "tp"),
        P(None, "tp"),
        P(None, "tp"),
        P("tp", None),
        P("grp", "seq", "tp", None, None),
        P("grp", "seq", "tp", None),
        P("grp", "seq", None, "tp"),
        P("grp", None),
        P(),
        P(),
    )
    return jax.shard_map(
        local, mesh=mesh, in_specs=placed, out_specs=P("grp", "seq", "tp"), check_vma=False
    )
```

time: 609 us -> 103 us (0.17)
  waiting for transfers between devices: 199 us -> 0 us
  blocking collectives: 173 us -> 0 us
  Pallas kernels: 0 us -> 87.2 us
  other arithmetic: 80.5 us -> 8.23 us
  local copies, waits for them, and re-layouts: 69.9 us -> 7.16 us
  matrix products: 40.2 us -> 0 us
  loops' own time: 22.1 us -> 0 us
  between operations: 16.7 us -> 0.03 us
    psum x1 -> x0, waiting for transfers between devices: 137 us -> none  [spread(): return lax.psum(kept, axis)]
    psum x1 -> x0, blocking collectives: 117 us -> none  [spread(): return lax.psum(kept, axis)]
    pallas_call x0 -> x4, Pallas kernels: none -> 87.2 us  [the longest x1 50 us: local(): pl.pallas_call(functools.partial(exchange_body, hd), out_shape=[shape((co...]
    reduce_scatter x1 -> x0, waiting for transfers between devices: 62.1 us -> none  [local(): summed = lax.psum_scatter(mixed_out, 'tp', scatter_dimension=1, tiled=True)]
    select_n x67 -> x0, other arithmetic: 61.2 us -> none  [the longest x64 58.2 us: step(): return jax.tree.map(lambda a, b: jnp.where(reached, a, b), new, before)]
    all_gather x3 -> x0, blocking collectives: 56.2 us -> none  [the longest x1 35.5 us: carried_in(): everything = jax.tree.map(lambda part: lax.all_gather(part, axis), shard)]
    dot_general x13 -> x0, matrix products: 40.2 us -> none  [the longest x1 5.51 us: local(): jnp.dot(normed, w_value, preferred_element_type=jnp.float32)]
    dynamic_slice x35 -> x2, local copies, waits for them, and re-layouts: 25.1 us -> 2.55 us  [local(): where = jnp.stack([prefix_owner[grp], row_group[grp]])]
  transfers between devices with their start and end apart: 5 -> 0, of which waited for: 2 -> 0; matrix products, arithmetic and copies ran while one was open for 16% -> 0% of each run, Pallas kernels for 0% -> 0%
where the time goes in v1:
time: 103 us
  Pallas kernels  87.2 us (85%)
  other arithmetic  8.23 us (8%)
  local copies, waits for them, and re-layouts  7.16 us (7%)
    pallas_call x1, Pallas kernels, local(): pl.pallas_call(functools.partial(exchange_body, hd), out_shape=[shape((co...  50 us
    pallas_call x1, Pallas kernels, local(): pl.pallas_call(project_body, out_shape=[shape((rows, heads * padded)), sh...  14.4 us
    pallas_call x1, Pallas kernels, local(): pl.pallas_call(output_body, out_shape=shape((rows, columns), f32), in_spe...  13.5 us
    pallas_call x1, Pallas kernels, local(): pl.pallas_call(functools.partial(attend_body, hd=hd, fd=fd), out_shape=sh...  9.26 us
    broadcast_in_dim x1, other arithmetic, local(): return (residual + mixed)[None]  2.93 us
    dynamic_slice x2, local copies, waits for them, and re-layouts, local(): where = jnp.stack([prefix_owner[grp], row_group[grp]])  2.55 us

profile of v1, /device:TPU:1, one launch (start us, length us, event | category | flops | bytes accessed | tf_op | source)
XLA Modules:
  0.0 102.6 jit_solution(14633214075344342337)
XLA Ops:
  0.0 1.2 %dynamic_slice.11 = s32[1]{0:T(128)} dynamic-slice(s32[4]{0:T(128)} %param.25, s32[]{:T(128)S(6)} %select_n.8), dynamic_slice_sizes={1} | dynamic-slice | bytes 12 | tf_op jit(solution)/shard_map/dynamic_slice | solution.py:376
  1.2 1.3 %dynamic_slice.10 = s32[1]{0:T(128)} dynamic-slice(s32[4]{0:T(128)} %param.24, s32[]{:T(128)S(6)} %select_n.8), dynamic_slice_sizes={1} | dynamic-slice | bytes 12 | tf_op jit(solution)/shard_map/dynamic_slice | solution.py:376
  2.6 2.0 %pad_add_fusion.where_ref = s32[2]{0:T(128)} fusion(s32[1]{0:T(128)} %dynamic_slice.11, s32[1]{0:T(128)} %dynamic_slice.10), kind=kLoop, calls=%fused_computation.4 | loop fusion | flops 2 | bytes 16 | tf_op jit(solution)/shard_map/stack | solution.py:376
  4.6 0.8 reduce-window.4
  5.4 1.2 %bitcast_subtract_fusion.1.starts_ref = s32[8]{0:T(128)} fusion(s32[1,8]{1,0:T(1,128)} %param.23, s32[8,1]{0,1:T(1,128)S(1)} %reduce-window.4), kind=kLoop, calls=%fused_computation.7 | loop fusion | flops 8 | bytes 96 | tf_op jit(solution)/shard_map/sub | solution.py:372
  6.6 0.7 fusion.1
  7.2 0.1 and_reduce_fusion
  7.3 0.6 convert_subtract_fusion.keep_ref
  7.9 1.3 %broadcast_in_dim.4.gain = f32[1,1792]{1,0:T(1,128)} reshape(f32[1792]{0:T(1024)} %param.15) | data formatting | bytes 14336 | tf_op jit(solution)/shard_map/broadcast_in_dim | solution.py:404
  9.2 1.7 %copy.21 = f32[1,1,4,153,112]{4,3,2,1,0:T(8,128)} copy(f32[1,1,4,153,112]{4,2,3,1,0:T(4,128)} %param.20) | data formatting | bytes 548352 | tf_op args[6]
  10.9 1.6 %copy.19.norm = f32[4,153,1]{2,1,0:T(8,128)} copy(f32[4,153,1]{1,0,2:T(4,128)} %bitcast.25) | data formatting | bytes 4896 | tf_op jit(solution)/shard_map/broadcast_in_dim;squeeze | solution.py:405
  12.5 14.4 %project.1 = (bf16[512,1024]{1,0:T(8,128)(2,1)}, bf16[512,128]{1,0:T(8,128)(2,1)}, bf16[128,512]{1,0:T(8,128)(2,1)}, bf16[4,512,128]{2,1,0:T(8,128)(2,1)}, bf16[...) custom-call(s32[8]{0:T(128)} %bitcast_subtract_fusion.1.starts_ref, ...), custom_call_target="tpu_custom_call" | custom-call | tf_op jit(solution)/shard_map/project/pallas_call | solution.py:386
  26.8 50.0 %exchange.1 = (bf16[32,48,128]{2,1,0:T(8,128)(2,1)}, bf16[32,32,128]{2,1,0:T(8,128)(2,1)}, bf16[8,64,128]{2,1,0:T(8,128)(2,1)}) custom-call(s32[2]{0:T(128)} %pad_add_fusion.where_ref, f32[32]{0:T(128)} %convert_subtract_fusion.keep_ref, bf16[32,48,128]{2,1,0:T(8,128)(2,1)} %get-tuple-element.22.cache, bf16[32,32,128]{2,1,0:T(8,128)(2,1)} %get-tuple-element.23.parts, ...), custom_call_target="tpu_custom_call" | custom-call | tf_op jit(solution)/shard_map/exchange/pallas_call | solution.py:409
  76.9 9.3 %attend.1.attended = bf16[512,1024]{1,0:T(8,128)(2,1)} custom-call(s32[8]{0:T(128)} %bitcast_subtract_fusion.1.starts_ref, bf16[512,1024]{1,0:T(8,128)(2,1)} %get-tuple-element.16.phi_q, bf16[512,128]{1,0:T(8,128)(2,1)} %get-tuple-element.17.feat, bf16[128,512]{1,0:T(8,128)(2,1)} %get-tuple-element.18.feat_t, ...), custom_call_target="tpu_custom_call" | custom-call | tf_op jit(solution)/shard_map/attend/pallas_call | solution.py:433
  86.1 0.0 copy-start
  86.1 13.5 %mix.1 = f32[512,896]{1,0:T(8,128)} custom-call(bf16[512,1024]{1,0:T(8,128)(2,1)} %attend.1.attended, bf16[896,1792]{1,0:T(8,128)(2,1)} %w_out.1), custom_call_target="tpu_custom_call" | custom-call | tf_op jit(solution)/shard_map/mix/pallas_call | solution.py:442
  99.7 0.0 copy-done
  99.7 2.9 %fusion = f32[1,512,896]{2,1,0:T(8,128)} fusion(f32[512,896]{1,0:T(8,128)} %mix.1, bf16[1,512,1792]{2,1,0:T(8,128)(2,1)S(1)} %copy-done, s32[]{:T(128)S(6)} %select_n.7), kind=kLoop, calls=%fused_computation.1 | loop fusion | flops 917504 | bytes 4587524 | tf_op jit(solution)/shard_map/broadcast_in_dim | solution.py:460
  (1 shorter events, 0.0 us)
Async XLA Ops:
  86.1 13.5 %copy-start = (bf16[1,512,1792]{2,1,0:T(8,128)(2,1)S(1)}, bf16[1,512,1792]{2,1,0:T(8,128)(2,1)}, u32[]{:S(2)}) copy-start(bf16[1,512,1792]{2,1,0:T(8,128)(2,1)} %param.14) | copy-start | bytes 5505028

commit v2 on v0

v2 whole, which is shorter than its diff:
```python
import functools
import math

import jax
import jax.numpy as jnp
import numpy as np
from jax import lax
from jax.experimental import pallas as pl
from jax.experimental.pallas import tpu as pltpu
from jax.sharding import PartitionSpec as P

MESH = pl.DeviceIdType.MESH
LANES = 128
NEAR = 4
CHUNK = 32
HIGH = 20
KV_CHUNK = 16
f32, bf16 = jnp.float32, jnp.bfloat16


def feature_tables(fd, chunks):
    first, second = np.triu_indices(fd)
    pair = 1 + fd + np.arange(len(first))
    order = np.concatenate(
        [[0], pair[first == second], 1 + np.arange(fd), pair[first != second]]
    ).astype(np.int64)
    rows = np.zeros((8, chunks * CHUNK), np.float32)
    rows[0:4] = -1.0
    rows[7] = -1.0
    for rank, feature in enumerate(order):
        chunk, at = rank % chunks, rank // chunks
        spots = [chunk * CHUNK + at]
        if at < CHUNK - HIGH:
            spots.append(chunk * CHUNK + HIGH + at)
        for spot in spots:
            rows[7, spot] = feature
            if feature == 0:
                rows[4:7, spot] = 1.0
            elif feature <= fd:
                rows[0, spot], rows[2, spot] = feature - 1, fd + feature - 1
                rows[5, spot], rows[6, spot] = 1.0, 1.0 / fd**0.25
            else:
                i, j = first[feature - 1 - fd], second[feature - 1 - fd]
                rows[0, spot], rows[1, spot] = i, j
                rows[2, spot], rows[3, spot] = fd + i, fd + j
                rows[6, spot] = 1.0 / math.sqrt(2.0 * fd if i == j else fd)
    return rows


def halves(x):
    hi = x.astype(bf16)
    return hi, (x - hi.astype(f32)).astype(bf16)


def dropped(x):
    return x - x.astype(bf16).astype(f32)


def places_of(shape):
    lane = lax.broadcasted_iota(jnp.int32, shape, 1)
    low = lax.broadcasted_iota(jnp.int32, shape, 0) % CHUNK >= HIGH
    return lane, low


def pack_new(x, hd):
    lane, low = places_of(x.shape)
    lost = dropped(x)
    high_rows = jnp.where(lane == hd + 1, pltpu.roll(lost, 1, 1), x)
    low_rows = jnp.where(lane < hd, lost, 0.0)
    return jnp.where(low, low_rows, high_rows).astype(bf16)


def pack_sum(x, hd):
    lane, low = places_of(x.shape)
    lost = dropped(x)
    x = jnp.where((lane == hd + 1) & ~low, x + pltpu.roll(lost, 1, 1), x)
    return jnp.where((lane < hd) & low, x + pltpu.roll(lost, HIGH, 0), x).astype(bf16)


def kernel(
    sizes,
    lengths, owners, groups, hidden_hbm, gain, w_feature, w_value_hbm, w_window_hbm, w_out,
    state, norm, kv, tab_row, tab_col,
    out,
    hidden, w_value, w_window, normed, wide, phi_q, feat, feat_t, lin_vals, win_q, win_kv, intra,
    cache, parts, got_near, quarter, got_far, mine, got_rows, base, got_parts, results, carried,
    rim, attended, from_other, w_own, w_other,
    load_sems, own_sems, w_send, w_recv, a_send, a_recv,
    near_out, near_in, far_out, far_in, row_out, row_in, bfar_out, bfar_in, bnear_out, bnear_in,
    part_out, part_in, res_out, res_in, rim_sems,
):
    heads, nf, hd, fd, count = sizes
    rows, width = hidden.shape
    span = rim.shape[1]
    half = out.shape[1]
    chunks = count // heads
    padded = chunks * CHUNK
    blocks = span // KV_CHUNK
    far = count // NEAR
    grp_count = got_rows.shape[0]
    row, me, core = lax.axis_index("grp"), lax.axis_index("seq"), lax.axis_index("tp")
    my_far, my_near = me // NEAR, me % NEAR
    other = 1 - core
    anchor = me * rows

    def remote(src, dst, send, recv, where):
        return pltpu.make_async_remote_copy(
            src_ref=src, dst_ref=dst, send_sem=send, recv_sem=recv,
            device_id=where, device_id_type=MESH,
        )

    def each_seq(do):
        def step(i, carry):
            off = count // 2 + ((i + 1) // 2) * (2 * (i % 2) - 1)
            do(lax.rem(me + off, count))
            return carry

        lax.fori_loop(0, count - 1, step, 0)

    def each_near(do):
        for i in (2, 1, 3):
            do(lax.rem(my_near + i, NEAR))

    def each_far(do):
        for i in (4, 3, 5, 2, 6, 1, 7):
            do(lax.rem(my_far + i, far))

    def each_row(do):
        for i in (2, 1, 3):
            do(lax.rem(row + i, grp_count))

    def near_copy(peer, slot):
        return remote(
            cache.at[pl.ds(peer * far, far)], got_near.at[slot], near_out.at[peer],
            near_in.at[slot], {"seq": my_far * NEAR + peer},
        )

    def far_copy(peer, slot):
        return remote(
            quarter.at[peer], got_far.at[slot], far_out.at[peer], far_in.at[slot],
            {"seq": peer * NEAR + my_near},
        )

    def row_copy(peer, slot):
        return remote(
            mine, got_rows.at[slot], row_out.at[peer], row_in.at[slot], {"grp": peer}
        )

    def base_far_copy(peer, slot):
        return remote(
            base.at[my_near * far + my_far], base.at[my_near * far + slot], bfar_out.at[peer],
            bfar_in.at[slot], {"seq": peer * NEAR + my_near},
        )

    def base_near_copy(peer, slot):
        return remote(
            base.at[pl.ds(my_near * far, far)], base.at[pl.ds(slot * far, far)],
            bnear_out.at[peer], bnear_in.at[slot], {"seq": my_far * NEAR + peer},
        )

    def part_copy(peer, slot):
        return remote(
            parts.at[peer], got_parts.at[slot], part_out.at[peer], part_in.at[slot],
            {"seq": peer},
        )

    def result_copy(peer, slot):
        return remote(
            results.at[peer], carried.at[slot], res_out.at[peer], res_in.at[slot],
            {"seq": peer},
        )

    def columns(which):
        return pl.ds(pl.multiple_of(which * half, LANES), half)

    loads = [
        pltpu.make_async_copy(hidden_hbm, hidden, load_sems.at[0]),
        pltpu.make_async_copy(w_value_hbm, w_value, load_sems.at[1]),
        pltpu.make_async_copy(w_window_hbm, w_window, load_sems.at[2]),
    ]
    for load in loads:
        load.start()
    own_w, sent_w, across = [], [], []
    for i in range(2 * heads):
        src, dst = slice(i * hd, (i + 1) * hd), slice(i * LANES, i * LANES + hd)
        own_w.append(
            pltpu.make_async_copy(w_out.at[src, columns(core)], w_own.at[dst, :], own_sems.at[i])
        )
        sent_w.append(
            remote(
                w_out.at[src, columns(other)], w_other.at[dst, :], w_send.at[i], w_recv.at[i],
                {"tp": other},
            )
        )
        tile = slice(i * LANES, (i + 1) * LANES)
        across.append(
            remote(
                attended.at[:, tile], from_other.at[:, tile], a_send.at[i], a_recv.at[i],
                {"tp": other},
            )
        )
    rim_copy = remote(
        win_kv.at[:, pl.ds(rows - span, span), :], rim, rim_sems.at[0], rim_sems.at[1],
        {"seq": lax.rem(me + 1, count)},
    )

    barrier = pltpu.get_barrier_semaphore()

    def greet(where):
        pl.semaphore_signal(barrier, inc=1, device_id=where, device_id_type=MESH)

    each_seq(lambda peer: greet({"seq": peer}))
    each_row(lambda peer: greet({"grp": peer}))
    greet({"tp": other})

    starts, total = [], jnp.int32(0)
    for r in range(lengths.shape[1]):
        starts.append(total)
        total = total + lengths[0, r]

    def start_of(place):
        best = jnp.int32(0)
        for start in starts:
            best = jnp.maximum(best, jnp.where(start <= place, start, 0))
        return best

    pick = jnp.where(
        lax.broadcasted_iota(jnp.int32, (padded, nf), 1).astype(f32) == tab_col[:, 7:8], 1.0, 0.0
    ).astype(bf16)
    norm_hi, norm_lo = halves(norm[...])
    contract = (((1,), (1,)), ((), ()))
    norms = lax.dot_general(pick, norm_hi, contract, preferred_element_type=f32)
    norms = norms + lax.dot_general(pick, norm_lo, contract, preferred_element_type=f32)
    for h in range(heads):
        hi, lo = halves(state[h])
        body = jnp.dot(pick, hi, preferred_element_type=f32)
        body = body + jnp.dot(pick, lo, preferred_element_type=f32)
        body = jnp.concatenate(
            [body, norms[:, h : h + 1], jnp.zeros((padded, LANES - hd - 1), f32)], axis=1
        )
        cache[h * chunks : (h + 1) * chunks, 0:CHUNK, :] = pack_new(body, hd).reshape(
            chunks, CHUNK, LANES
        )
    for i in range(2 * heads):
        piece = jnp.concatenate(
            [kv[:, i * hd : (i + 1) * hd], jnp.zeros((span, LANES - hd), bf16)], axis=1
        )
        cache[i * blocks : (i + 1) * blocks, CHUNK:, :] = piece.reshape(blocks, KV_CHUNK, LANES)
    for copy in own_w:
        copy.start()
    for i in range(2 * heads):
        rest = slice(i * LANES + hd, (i + 1) * LANES)
        w_own[rest, :] = jnp.zeros((LANES - hd, half), bf16)
        w_other[rest, :] = jnp.zeros((LANES - hd, half), bf16)

    loads[0].wait()
    step = 64
    scale = gain[...].reshape(1, width)

    def norm_rows(i, carry):
        at = pl.ds(pl.multiple_of(i * step, step), step)
        x = hidden[at, :].astype(f32)
        inv = lax.rsqrt(jnp.mean(x * x, axis=1, keepdims=True) + 1e-5)
        normed[at, :] = (x * inv * scale).astype(bf16)
        return carry

    lax.fori_loop(0, rows // step, norm_rows, 0)

    pl.semaphore_wait(barrier, count - 1 + grp_count - 1 + 1)
    each_near(lambda peer: near_copy(peer, my_near).start())
    got_near[my_near] = cache[pl.ds(my_near * far, far)]

    feats = jnp.dot(normed[...], w_feature[...], preferred_element_type=f32)
    both_t = jnp.concatenate(halves(jnp.transpose(feats)), axis=0)
    both = jnp.concatenate(halves(feats), axis=1)
    channels = feats.shape[1]
    feat[...] = both[:, 0:channels]
    feat_t[...] = both_t[0:channels, :]
    loads[1].wait()
    for lo in range(0, w_value.shape[1], 256):
        up = min(lo + 256, w_value.shape[1])
        wide[:, lo:up] = jnp.dot(
            normed[...], w_value[:, lo:up], preferred_element_type=f32
        ).astype(bf16)
    lane = lax.broadcasted_iota(jnp.int32, (rows, LANES - hd), 1)
    ones = jnp.where(lane == 0, 1.0, 0.0).astype(bf16)
    zeros = jnp.zeros((rows, LANES - hd), bf16)
    for h in range(heads):
        at = 2 * h * hd
        lin_vals[h] = jnp.concatenate([wide[:, at : at + hd], ones], axis=1)
    token = lax.broadcasted_iota(jnp.int32, (1, rows), 1)
    keep = jnp.where(token >= start_of(anchor + rows - 1) - anchor, 1.0, 0.0)
    for h in range(heads):
        channel = (
            lax.broadcasted_iota(jnp.int32, (padded, 2 * channels), 1) % channels - h * 2 * fd
        ).astype(f32)
        one = jnp.where((channel == tab_col[:, 2:3]) & (channel >= 0.0), 1.0, 0.0).astype(bf16)
        two = jnp.where((channel == tab_col[:, 3:4]) & (channel >= 0.0), 1.0, 0.0).astype(bf16)
        left = jnp.dot(one, both_t, preferred_element_type=f32) + tab_col[:, 4:5]
        right = jnp.dot(two, both_t, preferred_element_type=f32) + tab_col[:, 5:6]
        phi_t = (left * right * tab_col[:, 6:7] * keep).astype(bf16)
        own = jnp.dot(phi_t, lin_vals[h], preferred_element_type=f32)
        parts[h * chunks : (h + 1) * chunks] = pack_new(own, hd).reshape(chunks, CHUNK, LANES)
    each_seq(lambda peer: part_copy(peer, me).start())
    got_parts[me] = parts[me]

    owner = owners[row]
    each_near(lambda peer: near_copy(peer, peer).wait_recv())
    quarter[...] = got_near[owner % NEAR]
    each_far(lambda peer: far_copy(peer, my_far).start())
    got_far[my_far] = quarter[my_far]
    for copy in sent_w:
        copy.start()

    for h in range(heads):
        at = 2 * h * hd
        win_kv[2 * h + 1] = jnp.concatenate([wide[:, at + hd : at + 2 * hd], zeros], axis=1)
    loads[2].wait()
    for lo in range(0, w_window.shape[1], 256):
        up = min(lo + 256, w_window.shape[1])
        wide[:, lo:up] = jnp.dot(
            normed[...], w_window[:, lo:up], preferred_element_type=f32
        ).astype(bf16)
    for h in range(heads):
        at = 2 * h * hd
        win_q[h] = jnp.concatenate([wide[:, at : at + hd], zeros], axis=1)
        win_kv[2 * h] = jnp.concatenate([wide[:, at + hd : at + 2 * hd], zeros], axis=1)
    rim_copy.start()

    each_far(lambda peer: far_copy(peer, peer).wait_recv())
    mine[...] = got_far[owner // NEAR]
    each_row(lambda peer: row_copy(peer, row).start())
    got_rows[row] = mine[...]

    for h in range(heads):
        channel = (
            lax.broadcasted_iota(jnp.int32, (2 * channels, padded), 0) % channels - h * 2 * fd
        ).astype(f32)
        one = jnp.where((channel == tab_row[0:1, :]) & (channel >= 0.0), 1.0, 0.0).astype(bf16)
        two = jnp.where((channel == tab_row[1:2, :]) & (channel >= 0.0), 1.0, 0.0).astype(bf16)
        left = jnp.dot(both, one, preferred_element_type=f32) + tab_row[4:5, :]
        right = jnp.dot(both, two, preferred_element_type=f32) + tab_row[5:6, :]
        phi_q[:, h * padded : (h + 1) * padded] = (left * right * tab_row[6:7, :]).astype(bf16)

    each_row(lambda peer: row_copy(peer, peer).wait_recv())
    base[my_near * far + my_far] = got_rows[groups[row]]
    each_far(lambda peer: base_far_copy(peer, my_far).start())

    tile = 128
    begins = []
    for b in range(rows // tile):
        place = lax.broadcasted_iota(jnp.int32, (tile, 1), 0) + (b * tile + anchor)
        best = jnp.zeros((tile, 1), jnp.int32)
        for start in starts:
            best = jnp.maximum(best, jnp.where(start <= place, start, 0))
        begins.append(best - anchor)

    def within(b):
        first, seen = b * tile, (b + 1) * tile
        tokens = lax.broadcasted_iota(jnp.int32, (tile, 1), 0) + first
        key_at = lax.broadcasted_iota(jnp.int32, (tile, seen), 1)
        causal = (key_at <= tokens) & (key_at >= begins[b])
        for h in range(heads):
            q = feat[first:seen, h * 2 * fd : h * 2 * fd + fd]
            k_t = feat_t[h * 2 * fd + fd : (h + 1) * 2 * fd, 0:seen]
            similar = jnp.dot(q, k_t, preferred_element_type=f32) * (1.0 / math.sqrt(fd))
            mass = jnp.where(causal, 1.0 + similar + 0.5 * similar * similar, 0.0)
            intra[h, first:seen, :] = jnp.dot(
                mass.astype(bf16), lin_vals[h, 0:seen, :], preferred_element_type=f32
            )

    within(3)

    each_seq(lambda peer: part_copy(peer, peer).wait_recv())

    def scan(k, carry):
        results[k] = pack_sum(carry, hd)
        restart = start_of(k * rows + rows - 1) >= k * rows
        return carry * jnp.where(restart, 0.0, 1.0) + got_parts[k].astype(f32)

    lax.fori_loop(0, count, scan, jnp.zeros((CHUNK, LANES), f32))
    each_seq(lambda peer: result_copy(peer, me).start())
    carried[me] = results[me]

    each_far(lambda peer: base_far_copy(peer, peer).wait_recv())
    each_near(lambda peer: base_near_copy(peer, my_near).start())
    for b in range(3):
        within(b)

    each_near(lambda peer: base_near_copy(peer, peer).wait_recv())
    rim_copy.wait()
    for h in range(heads):
        for b in range(rows // tile):
            first = b * tile
            tokens = lax.broadcasted_iota(jnp.int32, (tile, 1), 0) + first
            slot = lax.broadcasted_iota(jnp.int32, (tile, 2 * span + tile), 1)
            near_at = slot + (first - 2 * span)
            early = (slot < span) & (slot >= tokens - begins[b] + 1)
            band = (
                (slot >= span) & (near_at <= tokens) & (near_at > tokens - span)
                & (near_at >= begins[b])
            )
            sides = []
            for i in (2 * h, 2 * h + 1):
                cached = base[i * blocks : (i + 1) * blocks, CHUNK:, :].reshape(span, LANES)
                if b == 0:
                    recent = [rim[i], win_kv[i, 0:tile, :]]
                else:
                    recent = [win_kv[i, first - span : first + tile, :]]
                sides.append(jnp.concatenate([cached] + recent, axis=0))
            scores = lax.dot_general(
                win_q[h, first : first + tile, :], sides[0], contract, preferred_element_type=f32
            ) * (1.0 / math.sqrt(hd))
            scores = jnp.where(early | band, scores, -1e30)
            weights = jnp.exp(scores - jnp.max(scores, axis=1, keepdims=True))
            weights = (weights / jnp.sum(weights, axis=1, keepdims=True)).astype(bf16)
            win_out = jnp.dot(weights, sides[1], preferred_element_type=f32)
            attended[first : first + tile, (2 * h + 1) * LANES : (2 * h + 2) * LANES] = (
                win_out.astype(bf16)
            )
        across[2 * h + 1].start()

    each_seq(lambda peer: result_copy(peer, peer).wait_recv())
    for h in range(heads):
        own = slice(h * chunks, (h + 1) * chunks)
        from_base = base[own, 0:CHUNK, :].reshape(padded, LANES)
        from_carry = carried[own].reshape(padded, LANES)
        for b in range(rows // tile):
            at = slice(b * tile, (b + 1) * tile)
            use_carry = jnp.where(begins[b] < 0, 1.0, 0.0)
            phi = phi_q[at, h * padded : (h + 1) * padded]
            mixed = intra[h, at, :] + jnp.dot(phi, from_base, preferred_element_type=f32)
            mixed = mixed + use_carry * jnp.dot(phi, from_carry, preferred_element_type=f32)
            below = mixed[:, hd : hd + 1] + mixed[:, hd + 1 : hd + 2]
            lane = lax.broadcasted_iota(jnp.int32, (tile, LANES), 1)
            attended[at, 2 * h * LANES : (2 * h + 1) * LANES] = jnp.where(
                lane < hd, mixed / below, 0.0
            ).astype(bf16)
        across[2 * h].start()

    for copy in own_w:
        copy.wait()
    for lo in range(0, half, 256):
        up = min(lo + 256, half)
        out[:, lo:up] = jnp.dot(attended[...], w_own[:, lo:up], preferred_element_type=f32)
    for copy in sent_w:
        copy.wait()
    for copy in across:
        copy.wait()
    for lo in range(0, half, 256):
        up = min(lo + 256, half)
        out[:, lo:up] += jnp.dot(from_other[...], w_other[:, lo:up], preferred_element_type=f32)
    each_near(lambda peer: near_copy(peer, my_near).wait_send())
    each_far(lambda peer: far_copy(peer, my_far).wait_send())
    each_row(lambda peer: row_copy(peer, row).wait_send())
    each_far(lambda peer: base_far_copy(peer, my_far).wait_send())
    each_near(lambda peer: base_near_copy(peer, my_near).wait_send())
    each_seq(lambda peer: part_copy(peer, me).wait_send())
    each_seq(lambda peer: result_copy(peer, me).wait_send())


def local(
    hidden_in, norm_gain, w_feature, w_value, w_window, w_out,
    prefix_state, prefix_norm, prefix_kv, lengths, prefix_owner, row_group,
):
    heads, nf, hd = prefix_state.shape[2:]
    fd = w_feature.shape[1] // (2 * heads)
    rows, width = hidden_in.shape[1:]
    span = prefix_kv.shape[2]
    count, groups = lax.axis_size("seq"), lax.axis_size("grp")
    far = count // NEAR
    chunks = count // heads
    columns = width // lax.axis_size("tp")
    tab = feature_tables(fd, chunks)
    both = CHUNK + KV_CHUNK
    dma = pltpu.SemaphoreType.DMA

    def pair(n):
        return [dma((n,)), dma((n,))]

    def vm(*dims, dtype=bf16):
        return pltpu.VMEM(dims, dtype)

    vmem = pl.BlockSpec(memory_space=pltpu.VMEM)
    smem = pl.BlockSpec(memory_space=pltpu.SMEM)
    anywhere = pl.BlockSpec(memory_space=pl.ANY)
    mixed = pl.pallas_call(
        functools.partial(kernel, (heads, nf, hd, fd, count)),
        out_shape=jax.ShapeDtypeStruct((rows, columns), f32),
        in_specs=[smem] * 3
        + [anywhere, vmem, vmem, anywhere, anywhere, anywhere]
        + [vmem] * 5,
        out_specs=vmem,
        scratch_shapes=[
            vm(rows, width), vm(width, 2 * heads * hd), vm(width, 2 * heads * hd),
            vm(rows, width), vm(rows, 2 * heads * hd),
            vm(rows, heads * chunks * CHUNK), vm(rows, 2 * heads * fd), vm(2 * heads * fd, rows),
            vm(heads, rows, LANES), vm(heads, rows, LANES), vm(2 * heads, rows, LANES),
            vm(heads, rows, LANES, dtype=f32),
            vm(count, both, LANES), vm(count, CHUNK, LANES),
            vm(NEAR, far, both, LANES), vm(far, both, LANES), vm(far, both, LANES),
            vm(both, LANES), vm(groups, both, LANES), vm(count, both, LANES),
            vm(count, CHUNK, LANES), vm(count, CHUNK, LANES), vm(count, CHUNK, LANES),
            vm(2 * heads, span, LANES),
            vm(rows, 2 * heads * LANES), vm(rows, 2 * heads * LANES),
            vm(2 * heads * LANES, columns), vm(2 * heads * LANES, columns),
            dma((3,)), dma((2 * heads,)),
        ]
        + pair(2 * heads) + pair(2 * heads)
        + pair(NEAR) + pair(far) + pair(groups) + pair(far) + pair(NEAR)
        + pair(count) + pair(count) + [dma((2,))],
        compiler_params=pltpu.CompilerParams(
            collective_id=0, has_side_effects=True, vmem_limit_bytes=60 * 1024 * 1024
        ),
        name="mixers",
    )(
        lengths, prefix_owner, row_group,
        hidden_in[0], norm_gain, w_feature, w_value, w_window, w_out,
        prefix_state[0, 0], prefix_norm[0, 0], prefix_kv[0, 0],
        jnp.asarray(tab), jnp.asarray(np.ascontiguousarray(tab.T)),
    )
    at = lax.axis_index("tp") * columns
    residual = lax.dynamic_slice_in_dim(hidden_in[0], at, columns, 1).astype(f32)
    return (residual + mixed)[None]


def solution(mesh):
    placed = (
        P("grp", "seq", None),
        P(),
        P(None, "tp"),
        P(None, "tp"),
        P(None, "tp"),
        P("tp", None),
        P("grp", "seq", "tp", None, None),
        P("grp", "seq", "tp", None),
        P("grp", "seq", None, "tp"),
        P("grp", None),
        P(),
        P(),
    )
    return jax.shard_map(
        local, mesh=mesh, in_specs=placed, out_specs=P("grp", "seq", "tp"), check_vma=False
    )
```

time: 609 us -> 60.7 us (0.10)
  waiting for transfers between devices: 199 us -> 0 us
  blocking collectives: 173 us -> 0 us
  other arithmetic: 80.5 us -> 2.92 us
  local copies, waits for them, and re-layouts: 69.9 us -> 1.72 us
  Pallas kernels: 0 us -> 55.9 us
  matrix products: 40.2 us -> 0 us
  loops' own time: 22.1 us -> 0 us
  between operations: 16.7 us -> 0.02 us
    psum x1 -> x0, waiting for transfers between devices: 137 us -> none  [spread(): return lax.psum(kept, axis)]
    psum x1 -> x0, blocking collectives: 117 us -> none  [spread(): return lax.psum(kept, axis)]
    reduce_scatter x1 -> x0, waiting for transfers between devices: 62.1 us -> none  [local(): summed = lax.psum_scatter(mixed_out, 'tp', scatter_dimension=1, tiled=True)]
    select_n x67 -> x0, other arithmetic: 61.2 us -> none  [the longest x64 58.2 us: step(): return jax.tree.map(lambda a, b: jnp.where(reached, a, b), new, before)]
    all_gather x3 -> x0, blocking collectives: 56.2 us -> none  [the longest x1 35.5 us: carried_in(): everything = jax.tree.map(lambda part: lax.all_gather(part, axis), shard)]
    pallas_call x0 -> x1, Pallas kernels: none -> 55.9 us  [local(): pl.pallas_call(functools.partial(kernel, (heads, nf, hd, fd, count)), out...]
    dot_general x13 -> x0, matrix products: 40.2 us -> none  [the longest x1 5.51 us: local(): jnp.dot(normed, w_value, preferred_element_type=jnp.float32)]
    dynamic_slice x35 -> x0, local copies, waits for them, and re-layouts: 25.1 us -> none  [the longest x32 20.7 us: step(): new = combine(before, jax.tree.map(lambda part: part[k], everything))]
  transfers between devices with their start and end apart: 5 -> 0, of which waited for: 2 -> 0; matrix products, arithmetic and copies ran while one was open for 16% -> 0% of each run, Pallas kernels for 0% -> 0%
where the time goes in v2:
time: 60.7 us; the launch traced here: 60.6 us
  Pallas kernels  55.9 us (92%)
  other arithmetic  2.92 us (5%)
  local copies, waits for them, and re-layouts  1.72 us (3%)
    pallas_call x1, Pallas kernels, local(): pl.pallas_call(functools.partial(kernel, (heads, nf, hd, fd, count)), out...  55.9 us
    broadcast_in_dim x1, other arithmetic, local(): return (residual + mixed)[None]  2.92 us
    unnamed x3, local copies, waits for them, and re-layouts  1.72 us

profile of v2, /device:TPU:1, one launch (start us, length us, event | category | flops | bytes accessed | tf_op | source)
XLA Modules:
  0.0 60.6 jit_solution(8371740094158134341)
XLA Ops:
  0.0 1.7 %copy.17 = f32[1,1,4,153,112]{4,3,2,1,0:T(8,128)} copy(f32[1,1,4,153,112]{4,2,3,1,0:T(4,128)} %param.20) | data formatting | bytes 548352 | tf_op args[6]
  1.7 0.0 copy-start
  1.7 55.9 %mixers.1 = f32[512,896]{1,0:T(8,128)} custom-call(s32[1,8]{1,0:T(1,128)} %lengths.1, s32[4]{0:T(128)} %owners.1, s32[4]{0:T(128)} %groups.1, bf16[512,1792]{1,0:T(8,128)(2,1)} %bitcast.11, f32[1792]{0:T(1024)} %gain.1, bf16[1792,128]{1,0:T(8,128)(2,1)} %w_feature.1, bf16[1792,896]{1,0:T(8,128)(2,1)} %w_value_hbm.1, bf16[1792,896]{1,0:T(8,128)(2,1)} %w_window_hbm.1, ...), custom_call_target="tpu_custom_call" | custom-call | tf_op jit(solution)/shard_map/mixers/pallas_call | solution.py:487
  57.6 0.0 copy-done
  57.6 2.9 %fusion = f32[1,512,896]{2,1,0:T(8,128)} fusion(f32[512,896]{1,0:T(8,128)} %mixers.1, bf16[1,512,1792]{2,1,0:T(8,128)(2,1)S(1)} %copy-done, s32[]{:T(128)S(6)} %select_n.3), kind=kLoop, calls=%fused_computation.1 | loop fusion | flops 917504 | bytes 4587524 | tf_op jit(solution)/shard_map/broadcast_in_dim | solution.py:524
Async XLA Ops:
  1.7 55.9 %copy-start = (bf16[1,512,1792]{2,1,0:T(8,128)(2,1)S(1)}, bf16[1,512,1792]{2,1,0:T(8,128)(2,1)}, u32[]{:S(2)}) copy-start(bf16[1,512,1792]{2,1,0:T(8,128)(2,1)} %param.14) | copy-start | bytes 5505028

commit v3 on v2

--- a/solution.py
+++ b/solution.py
@@ -12,7 +12,7 @@
 MESH = pl.DeviceIdType.MESH
 LANES = 128
 NEAR = 4
-CHUNK = 32
+CHUNK = 24
 HIGH = 20
 KV_CHUNK = 16
 f32, bf16 = jnp.float32, jnp.bfloat16
@@ -79,14 +79,14 @@
 
 def kernel(
     sizes,
-    lengths, owners, groups, hidden_hbm, gain, w_feature, w_value_hbm, w_window_hbm, w_out,
-    state, norm, kv, tab_row, tab_col,
+    lengths, owners, groups, hidden_hbm, gain, w_feature_hbm, w_value_hbm, w_window_hbm, w_out,
+    state_hbm, norm, kv_hbm, tab_row, tab_col,
     out,
-    hidden, w_value, w_window, normed, wide, phi_q, feat, feat_t, lin_vals, win_q, win_kv, intra,
+    restarts, state, kv, hidden, w_feature, w_value, w_window, normed, wide, phi_q, feat, feat_t, lin_vals, win_q, win_kv, intra,
     cache, parts, got_near, quarter, got_far, mine, got_rows, base, got_parts, results, carried,
     rim, attended, from_other, w_own, w_other,
     load_sems, own_sems, w_send, w_recv, a_send, a_recv,
-    near_out, near_in, far_out, far_in, row_out, row_in, bfar_out, bfar_in, bnear_out, bnear_in,
+    near_out, near_in, far_out, far_in, row_out, row_in, bfar_out, bfar_in, slab_out, slab_in,
     part_out, part_in, res_out, res_in, rim_sems,
 ):
     heads, nf, hd, fd, count = sizes
@@ -152,11 +152,37 @@
             bfar_in.at[slot], {"seq": peer * NEAR + my_near},
         )
 
-    def base_near_copy(peer, slot):
-        return remote(
-            base.at[pl.ds(my_near * far, far)], base.at[pl.ds(slot * far, far)],
-            bnear_out.at[peer], bnear_in.at[slot], {"seq": my_far * NEAR + peer},
-        )
+    kinds = (slice(0, KV_CHUNK), slice(KV_CHUNK, KV_CHUNK + CHUNK))
+    east, west = lax.rem(my_near + 1, NEAR), lax.rem(my_near + NEAR - 1, NEAR)
+
+    def slab_copies(kind, forward):
+        copies = []
+        for way, peer in enumerate((east, west)):
+            first, size = my_near * far, far
+            if forward:
+                first, size = (west, east)[way] * far + way * (far // 2), far // 2
+            part = base.at[pl.ds(first, size), kinds[kind], :]
+            at = 4 * forward + 2 * kind + way
+            copies.append(
+                remote(
+                    part, part, slab_out.at[at], slab_in.at[at], {"seq": my_far * NEAR + peer}
+                )
+            )
+        return copies
+
+    slabs = {(kind, forward): slab_copies(kind, forward) for kind in (0, 1) for forward in (0, 1)}
+
+    def slab_arrived(kind, forward):
+        for way in range(2):
+            first, size = (west, east)[way] * far, far
+            if forward:
+                first, size = lax.rem(my_near + 2, NEAR) * far + way * (far // 2), far // 2
+            part = base.at[pl.ds(first, size), kinds[kind], :]
+            at = 4 * forward + 2 * kind + way
+            remote(
+                part, part, slab_out.at[at], slab_in.at[at],
+                {"seq": my_far * NEAR + (east, west)[way]},
+            ).wait_recv()
 
     def part_copy(peer, slot):
         return remote(
@@ -175,9 +201,14 @@
 
     loads = [
         pltpu.make_async_copy(hidden_hbm, hidden, load_sems.at[0]),
-        pltpu.make_async_copy(w_value_hbm, w_value, load_sems.at[1]),
-        pltpu.make_async_copy(w_window_hbm, w_window, load_sems.at[2]),
+        pltpu.make_async_copy(w_feature_hbm, w_feature, load_sems.at[1]),
+        pltpu.make_async_copy(w_value_hbm, w_value, load_sems.at[2]),
+        pltpu.make_async_copy(kv_hbm, kv, load_sems.at[3]),
+    ] + [
+        pltpu.make_async_copy(state_hbm.at[:, h, :], state.at[h], load_sems.at[4 + h])
+        for h in range(heads)
     ]
+    last_load = pltpu.make_async_copy(w_window_hbm, w_window, load_sems.at[4 + heads])
     for load in loads:
         load.start()
     own_w, sent_w, across = [], [], []
@@ -224,36 +255,14 @@
             best = jnp.maximum(best, jnp.where(start <= place, start, 0))
         return best
 
-    pick = jnp.where(
-        lax.broadcasted_iota(jnp.int32, (padded, nf), 1).astype(f32) == tab_col[:, 7:8], 1.0, 0.0
-    ).astype(bf16)
-    norm_hi, norm_lo = halves(norm[...])
-    contract = (((1,), (1,)), ((), ()))
-    norms = lax.dot_general(pick, norm_hi, contract, preferred_element_type=f32)
-    norms = norms + lax.dot_general(pick, norm_lo, contract, preferred_element_type=f32)
-    for h in range(heads):
-        hi, lo = halves(state[h])
-        body = jnp.dot(pick, hi, preferred_element_type=f32)
-        body = body + jnp.dot(pick, lo, preferred_element_type=f32)
-        body = jnp.concatenate(
-            [body, norms[:, h : h + 1], jnp.zeros((padded, LANES - hd - 1), f32)], axis=1
-        )
-        cache[h * chunks : (h + 1) * chunks, 0:CHUNK, :] = pack_new(body, hd).reshape(
-            chunks, CHUNK, LANES
-        )
-    for i in range(2 * heads):
-        piece = jnp.concatenate(
-            [kv[:, i * hd : (i + 1) * hd], jnp.zeros((span, LANES - hd), bf16)], axis=1
-        )
-        cache[i * blocks : (i + 1) * blocks, CHUNK:, :] = piece.reshape(blocks, KV_CHUNK, LANES)
-    for copy in own_w:
-        copy.start()
-    for i in range(2 * heads):
-        rest = slice(i * LANES + hd, (i + 1) * LANES)
-        w_own[rest, :] = jnp.zeros((LANES - hd, half), bf16)
-        w_other[rest, :] = jnp.zeros((LANES - hd, half), bf16)
+    def note(k, carry):
+        restarts[k] = jnp.where(start_of(k * rows + rows - 1) >= k * rows, 0.0, 1.0)
+        return carry
+
+    lax.fori_loop(0, count, note, 0)
 
     loads[0].wait()
+    last_load.start()
     step = 64
     scale = gain[...].reshape(1, width)
 
@@ -266,17 +275,45 @@
 
     lax.fori_loop(0, rows // step, norm_rows, 0)
 
-    pl.semaphore_wait(barrier, count - 1 + grp_count - 1 + 1)
-    each_near(lambda peer: near_copy(peer, my_near).start())
-    got_near[my_near] = cache[pl.ds(my_near * far, far)]
-
+    pick = jnp.where(
+        lax.broadcasted_iota(jnp.int32, (padded, nf), 1).astype(f32) == tab_col[:, 7:8], 1.0, 0.0
+    ).astype(bf16)
+    for load in loads[3:]:
+        load.wait()
+    norm_hi, norm_lo = halves(norm[...])
+    contract = (((1,), (1,)), ((), ()))
+    norms = lax.dot_general(pick, norm_hi, contract, preferred_element_type=f32)
+    norms = norms + lax.dot_general(pick, norm_lo, contract, preferred_element_type=f32)
+    for h in range(heads):
+        hi, lo = halves(state[h])
+        body = jnp.dot(pick, hi, preferred_element_type=f32)
+        body = body + jnp.dot(pick, lo, preferred_element_type=f32)
+        body = jnp.concatenate(
+            [body, norms[:, h : h + 1], jnp.zeros((padded, LANES - hd - 1), f32)], axis=1
+        )
+        cache[h * chunks : (h + 1) * chunks, KV_CHUNK:, :] = pack_new(body, hd).reshape(
+            chunks, CHUNK, LANES
+        )
+    for i in range(2 * heads):
+        piece = jnp.concatenate(
+            [kv[:, i * hd : (i + 1) * hd], jnp.zeros((span, LANES - hd), bf16)], axis=1
+        )
+        cache[i * blocks : (i + 1) * blocks, 0:KV_CHUNK, :] = piece.reshape(blocks, KV_CHUNK, LANES)
+    for i in range(2 * heads):
+        rest = slice(i * LANES + hd, (i + 1) * LANES)
+        w_own[rest, :] = jnp.zeros((LANES - hd, half), bf16)
+        w_other[rest, :] = jnp.zeros((LANES - hd, half), bf16)
+
+    loads[1].wait()
     feats = jnp.dot(normed[...], w_feature[...], preferred_element_type=f32)
     both_t = jnp.concatenate(halves(jnp.transpose(feats)), axis=0)
     both = jnp.concatenate(halves(feats), axis=1)
     channels = feats.shape[1]
     feat[...] = both[:, 0:channels]
     feat_t[...] = both_t[0:channels, :]
-    loads[1].wait()
+    loads[2].wait()
+    for copy in own_w:
+        copy.start()
     for lo in range(0, w_value.shape[1], 256):
         up = min(lo + 256, w_value.shape[1])
         wide[:, lo:up] = jnp.dot(
@@ -288,6 +325,10 @@
     for h in range(heads):
         at = 2 * h * hd
         lin_vals[h] = jnp.concatenate([wide[:, at : at + hd], ones], axis=1)
+    pl.semaphore_wait(barrier, count - 1 + grp_count - 1 + 1)
+    each_near(lambda peer: near_copy(peer, my_near).start())
+    got_near[my_near] = cache[pl.ds(my_near * far, far)]
+
     token = lax.broadcasted_iota(jnp.int32, (1, rows), 1)
     keep = jnp.where(token >= start_of(anchor + rows - 1) - anchor, 1.0, 0.0)
     for h in range(heads):
@@ -315,7 +356,7 @@
     for h in range(heads):
         at = 2 * h * hd
         win_kv[2 * h + 1] = jnp.concatenate([wide[:, at + hd : at + 2 * hd], zeros], axis=1)
-    loads[2].wait()
+    last_load.wait()
     for lo in range(0, w_window.shape[1], 256):
         up = min(lo + 256, w_window.shape[1])
         wide[:, lo:up] = jnp.dot(
@@ -373,21 +414,30 @@
 
     each_seq(lambda peer: part_copy(peer, peer).wait_recv())
 
-    def scan(k, carry):
-        results[k] = pack_sum(carry, hd)
-        restart = start_of(k * rows + rows - 1) >= k * rows
-        return carry * jnp.where(restart, 0.0, 1.0) + got_parts[k].astype(f32)
-
-    lax.fori_loop(0, count, scan, jnp.zeros((CHUNK, LANES), f32))
+    def scan(i, carry):
+        for j in range(8):
+            k = i * 8 + j
+            results[k] = pack_sum(carry, hd)
+            carry = carry * restarts[k] + got_parts[k].astype(f32)
+        return carry
+
+    lax.fori_loop(0, count // 8, scan, jnp.zeros((CHUNK, LANES), f32))
     each_seq(lambda peer: result_copy(peer, me).start())
     carried[me] = results[me]
 
     each_far(lambda peer: base_far_copy(peer, peer).wait_recv())
-    each_near(lambda peer: base_near_copy(peer, my_near).start())
-    for b in range(3):
-        within(b)
-
-    each_near(lambda peer: base_near_copy(peer, peer).wait_recv())
+    for kind in range(2):
+        for copy in slabs[kind, 0]:
+            copy.start()
+    within(0)
+    within(1)
+    for kind in range(2):
+        slab_arrived(kind, 0)
+        for copy in slabs[kind, 1]:
+            copy.start()
+    within(2)
+
+    slab_arrived(0, 1)
     rim_copy.wait()
     for h in range(heads):
         for b in range(rows // tile):
@@ -402,7 +452,7 @@
             )
             sides = []
             for i in (2 * h, 2 * h + 1):
-                cached = base[i * blocks : (i + 1) * blocks, CHUNK:, :].reshape(span, LANES)
+                cached = base[i * blocks : (i + 1) * blocks, 0:KV_CHUNK, :].reshape(span, LANES)
                 if b == 0:
                     recent = [rim[i], win_kv[i, 0:tile, :]]
                 else:
@@ -420,10 +470,11 @@
             )
         across[2 * h + 1].start()
 
+    slab_arrived(1, 1)
     each_seq(lambda peer: result_copy(peer, peer).wait_recv())
     for h in range(heads):
         own = slice(h * chunks, (h + 1) * chunks)
-        from_base = base[own, 0:CHUNK, :].reshape(padded, LANES)
+        from_base = base[own, KV_CHUNK:, :].reshape(padded, LANES)
         from_carry = carried[own].reshape(padded, LANES)
         for b in range(rows // tile):
             at = slice(b * tile, (b + 1) * tile)
@@ -442,7 +493,10 @@
         copy.wait()
     for lo in range(0, half, 256):
         up = min(lo + 256, half)
-        out[:, lo:up] = jnp.dot(attended[...], w_own[:, lo:up], preferred_element_type=f32)
+        residual = hidden[:, pl.ds(pl.multiple_of(core * half + lo, LANES), up - lo)].astype(f32)
+        out[:, lo:up] = residual + jnp.dot(
+            attended[...], w_own[:, lo:up], preferred_element_type=f32
+        )
     for copy in sent_w:
         copy.wait()
     for copy in across:
@@ -454,7 +508,9 @@
     each_far(lambda peer: far_copy(peer, my_far).wait_send())
     each_row(lambda peer: row_copy(peer, row).wait_send())
     each_far(lambda peer: base_far_copy(peer, my_far).wait_send())
-    each_near(lambda peer: base_near_copy(peer, my_near).wait_send())
+    for copies in slabs.values():
+        for copy in copies:
+            copy.wait_send()
     each_seq(lambda peer: part_copy(peer, me).wait_send())
     each_seq(lambda peer: result_copy(peer, me).wait_send())
 
@@ -488,11 +544,12 @@
         functools.partial(kernel, (heads, nf, hd, fd, count)),
         out_shape=jax.ShapeDtypeStruct((rows, columns), f32),
         in_specs=[smem] * 3
-        + [anywhere, vmem, vmem, anywhere, anywhere, anywhere]
-        + [vmem] * 5,
+        + [anywhere, vmem] + [anywhere] * 5 + [vmem, anywhere, vmem, vmem],
         out_specs=vmem,
         scratch_shapes=[
-            vm(rows, width), vm(width, 2 * heads * hd), vm(width, 2 * heads * hd),
+            pltpu.SMEM((count,), f32), vm(heads, nf, hd, dtype=f32), vm(span, 2 * heads * hd),
+            vm(rows, width), vm(width, 2 * heads * fd),
+            vm(width, 2 * heads * hd), vm(width, 2 * heads * hd),
             vm(rows, width), vm(rows, 2 * heads * hd),
             vm(rows, heads * chunks * CHUNK), vm(rows, 2 * heads * fd), vm(2 * heads * fd, rows),
             vm(heads, rows, LANES), vm(heads, rows, LANES), vm(2 * heads, rows, LANES),
@@ -504,10 +561,10 @@
             vm(2 * heads, span, LANES),
             vm(rows, 2 * heads * LANES), vm(rows, 2 * heads * LANES),
             vm(2 * heads * LANES, columns), vm(2 * heads * LANES, columns),
-            dma((3,)), dma((2 * heads,)),
+            dma((5 + heads,)), dma((2 * heads,)),
         ]
         + pair(2 * heads) + pair(2 * heads)
-        + pair(NEAR) + pair(far) + pair(groups) + pair(far) + pair(NEAR)
+        + pair(NEAR) + pair(far) + pair(groups) + pair(far) + pair(8)
         + pair(count) + pair(count) + [dma((2,))],
         compiler_params=pltpu.CompilerParams(
             collective_id=0, has_side_effects=True, vmem_limit_bytes=60 * 1024 * 1024
@@ -516,12 +573,10 @@
     )(
         lengths, prefix_owner, row_group,
         hidden_in[0], norm_gain, w_feature, w_value, w_window, w_out,
-        prefix_state[0, 0], prefix_norm[0, 0], prefix_kv[0, 0],
+        jnp.swapaxes(prefix_state[0, 0], 0, 1), prefix_norm[0, 0], prefix_kv[0, 0],
         jnp.asarray(tab), jnp.asarray(np.ascontiguousarray(tab.T)),
     )
-    at = lax.axis_index("tp") * columns
-    residual = lax.dynamic_slice_in_dim(hidden_in[0], at, columns, 1).astype(f32)
-    return (residual + mixed)[None]
+    return mixed[None]
 
 
 def solution(mesh):

time: 60.7 us -> 58.6 us (0.965)
  other arithmetic: 2.92 us -> 0 us
  local copies, waits for them, and re-layouts: 1.72 us -> 2.85 us
    broadcast_in_dim x1 -> x0, other arithmetic: 2.92 us -> none  [local(): return (residual + mixed)[None]]
    unnamed x3 -> x1, local copies, waits for them, and re-layouts: 1.72 us -> 2.85 us
where the time goes in v3:
time: 58.6 us; the launch traced here: 58.5 us
  Pallas kernels  55.6 us (95%)
  local copies, waits for them, and re-layouts  2.85 us (5%)
    pallas_call x1, Pallas kernels, local(): pl.pallas_call(functools.partial(kernel, (heads, nf, hd, fd, count)), out...  55.6 us
    unnamed x1, local copies, waits for them, and re-layouts  2.85 us

profile of v3, /device:TPU:1, one launch (start us, length us, event | category | flops | bytes accessed | tf_op | source)
XLA Modules:
  0.0 58.5 jit_solution(2003856617085888099)
XLA Ops:
  0.0 55.6 %mixers.1 = f32[512,896]{1,0:T(8,128)} custom-call(s32[1,8]{1,0:T(1,128)} %lengths.1, s32[4]{0:T(128)} %owners.1, s32[4]{0:T(128)} %groups.1, bf16[512,1792]{1,0:T(8,128)(2,1)} %bitcast.8, f32[1792]{0:T(1024)} %gain.1, bf16[1792,128]{1,0:T(8,128)(2,1)} %w_feature_hbm.1, bf16[1792,896]{1,0:T(8,128)(2,1)} %w_value_hbm.1, bf16[1792,896]{1,0:T(8,128)(2,1)} %w_window_hbm.1, ...), custom_call_target="tpu_custom_call" | custom-call | tf_op jit(solution)/shard_map/mixers/pallas_call | solution.py:543
  55.6 2.8 %copy.16 = f32[1,512,896]{2,1,0:T(8,128)} copy(f32[1,512,896]{2,1,0:T(8,128)} %bitcast.7) | data formatting | bytes 3670016
